TPU v7x, 256 devices: a whole 4x4x8 slice. The times are simulated.
256 devices in a mesh: grp: 16 (over z_lo, x), own: 16 (over z_hi, y, core).
Axes of the slice: x: 4, y: 4, z: 8 (z_hi: 2, z_lo: 4; z = z_hi * 4 + z_lo), core: 2. Of those that a mesh axis runs over, the one named last changes fastest.
Arguments:
- vectors: float32 [16, 64, 2048], P('own'), may hold values from -6 to 6
- tiles: float32 [16, 16, 128, 128, 128], P('grp', 'own'), may hold values from -0.046875 to 0.046875
- tile_rows: int32 [16, 16, 128], P('grp', 'own'), may hold values from 0 to 15
- tile_cols: int32 [16, 16, 128], P('grp', 'own'), may hold values from 0 to 63
- tile_counts: int32 [16, 16], P('grp', 'own'), may hold values from 16 to 128, as said below
- matchings: int32 [16, 3], P('grp'), may hold values from 1 to 15, as said below
Outputs:
- products: float32 [16, 64, 2048], P('own', None, 'grp')
Inputs may be any that keep to these rules, and one draw needn't show every extreme that they name: `tile_counts`: the largest value 128 is held by some device in every draw. Each row holds 3 different values; matching j of part g pairs owner o with owner o XOR matchings[g, j].
All inputs are finite; a program needn't handle non-finite values.
Results may differ from a plain program's by a relative error of at most 0.0003.
Values sent between devices are 32-bit elements; how exact they have to be, the bound alone decides.
No kernel may reach another device: no remote copies, remote signals or barrier semaphores. Data moves between devices by JAX's collectives and lax.ppermute only.
A program may use at most 64 MiB of HBM per device.

v0:
```python
import jax
import jax.numpy as jnp
from jax import lax
from jax.experimental import pallas as pl
from jax.experimental.pallas import tpu as pltpu
from jax.sharding import Mesh, PartitionSpec as P

ZLO, X, ZHI, Y, CORE = 4, 4, 2, 4, 2
YC = Y * CORE
OWN = ZHI * YC
FAN = X * YC
GRP_AXES = ("zlo", "x")
OWN_AXES = ("zhi", "y", "core")
FAN_AXES = ("x", "y", "core")
OUT_AXES = ("zlo", "zhi", "y", "core")

REGIONS = 4
SUB = 8
LANE = 128
CHUNK = 16
GROUP = 4

VMEM = pl.BlockSpec(memory_space=pltpu.VMEM)
SMEM = pl.BlockSpec(memory_space=pltpu.SMEM)
ANY = pl.BlockSpec(memory_space=pl.ANY)

BY_COLS = (((1,), (0,)), ((), ()))
BY_ROWS = (((1,), (1,)), ((), ()))


def halves(value):
    high = value.astype(jnp.bfloat16)
    return high, (value - high.astype(jnp.float32)).astype(jnp.bfloat16)


def product(pair, high, low, dims):
    both = jnp.concatenate([high, low], axis=1 if dims is BY_COLS else 0)
    wide = lax.dot_general(pair, both, dims, preferred_element_type=jnp.float32)
    count = pair.shape[0] // 2
    return wide[:count, :LANE] + wide[count:, :LANE] + wide[:count, LANE:]


def pieces_kernel(x_ref, own_ref, out_ref):
    x = x_ref[0]
    for zlo in range(ZLO):
        start = pl.multiple_of((zlo * X + x) * LANE, LANE)
        for part in range(YC):
            block = own_ref[part * SUB : (part + 1) * SUB, pl.ds(start, LANE)]
            for zhi in range(ZHI):
                out_ref[zhi * YC + part, zlo] = block


def route_kernel(x_ref, zhi_ref, m0, m1, m2, m3, pieces_ref, out_ref):
    x = x_ref[0]
    first = zhi_ref[0] * YC
    for step, masks in enumerate((m0, m1, m2, m3)):
        base = lax.rem(x + step, X) * YC
        for slot in range(REGIONS - 1):
            mask = masks[0, slot]
            for part in range(YC):
                out_ref[base + part, slot] = pieces_ref[(first + part) ^ mask]


def collect_kernel(x_ref, zhi_ref, m0, m1, m2, m3, parts_ref, out_ref):
    x = x_ref[0]
    first = zhi_ref[0] * YC
    out_ref[...] = jnp.zeros_like(out_ref)
    for step, masks in enumerate((m0, m1, m2, m3)):
        base = lax.rem(x + step, X) * YC
        for slot in range(REGIONS):
            for part in range(YC):
                owner = first + part
                if slot > 0:
                    owner = owner ^ masks[0, slot - 1]
                for zlo in range(ZLO):
                    out_ref[zlo, owner] += parts_ref[base + part, slot, zlo]


def products_kernel(rows, cols, count, tiles, own_ref, far_ref, out_ref, held, table, sems):
    chunks = held.shape[0] // CHUNK
    copies = [
        pltpu.make_async_copy(
            tiles.at[pl.ds(i * CHUNK, CHUNK)], held.at[pl.ds(i * CHUNK, CHUNK)], sems.at[i]
        )
        for i in range(chunks)
    ]
    for copy in copies:
        copy.start()
    out_ref[...] = jnp.zeros_like(out_ref)
    vecs = own_ref.shape[0]
    blocks = own_ref.shape[1] // LANE
    for block in range(blocks):
        high, low = halves(own_ref[:, block * LANE : (block + 1) * LANE])
        table[block, :vecs] = high
        table[block, vecs:] = low
    for slot in range(REGIONS - 1):
        for block in range(blocks):
            value = jnp.concatenate(
                [far_ref[block % X * YC + part, slot, block // X] for part in range(YC)], axis=0
            )
            high, low = halves(value)
            table[(slot + 1) * blocks + block, :vecs] = high
            table[(slot + 1) * blocks + block, vecs:] = low
    live = count[0]

    def add(region, block, value):
        zlo = block // X
        base = lax.rem(block, X) * YC
        for part in range(YC):
            out_ref[base + part, region, zlo] += value[part * SUB : (part + 1) * SUB]

    def group(first, size):
        sums = []
        for k in range(size):
            row = rows[first + k]
            col = cols[first + k]
            high, low = halves(held[first + k])
            sums.append(
                (
                    row,
                    col,
                    product(table[col], high, low, BY_ROWS),
                    product(table[row], high, low, BY_COLS),
                )
            )
        for row, col, by_rows, by_cols in sums:
            add(0, row, by_rows)
            add(col // blocks, lax.rem(col, blocks), by_cols)

    for i, copy in enumerate(copies):
        copy.wait()
        here = jnp.clip(live - i * CHUNK, 0, CHUNK)
        full = here // GROUP

        def several(step, carry, i=i):
            group(i * CHUNK + step * GROUP, GROUP)
            return carry

        def single(step, carry, i=i):
            group(i * CHUNK + step, 1)
            return carry

        lax.fori_loop(0, full, several, 0)
        lax.fori_loop(full * GROUP, here, single, 0)


def exchange(value, axes):
    return lax.all_to_all(value, axes, 0, 0, tiled=False)


def on_device(vectors, tiles, tile_rows, tile_cols, tile_counts, matchings):
    own = vectors[0]
    tile_set = tiles[0, 0]
    vecs = own.shape[0]
    x = lax.axis_index("x").reshape(1).astype(jnp.int32)
    zhi = lax.axis_index("zhi").reshape(1).astype(jnp.int32)
    masks = [matchings] + [
        lax.ppermute(matchings, "x", [(i, (i - step) % X) for i in range(X)])
        for step in range(1, X)
    ]
    where = (x, zhi, *masks)
    piece = (ZLO, SUB, LANE)
    pieces = pl.pallas_call(
        pieces_kernel,
        out_shape=jax.ShapeDtypeStruct((OWN, *piece), jnp.float32),
        in_specs=[SMEM, VMEM],
        out_specs=VMEM,
        name="pieces",
    )(x, own)
    pieces = exchange(pieces, OWN_AXES)
    wanted = pl.pallas_call(
        route_kernel,
        out_shape=jax.ShapeDtypeStruct((FAN, REGIONS - 1, *piece), jnp.float32),
        in_specs=[SMEM] * 6 + [VMEM],
        out_specs=VMEM,
        name="route",
    )(*where, pieces)
    far = exchange(wanted, FAN_AXES)
    parts = pl.pallas_call(
        products_kernel,
        out_shape=jax.ShapeDtypeStruct((FAN, REGIONS, *piece), jnp.float32),
        in_specs=[SMEM] * 3 + [ANY, VMEM, VMEM],
        out_specs=VMEM,
        scratch_shapes=[
            pltpu.VMEM(tile_set.shape, jnp.float32),
            pltpu.VMEM((REGIONS * own.shape[1] // LANE, 2 * vecs, LANE), jnp.bfloat16),
            pltpu.SemaphoreType.DMA((tile_set.shape[0] // CHUNK,)),
        ],
        name="products",
    )(tile_rows[0, 0], tile_cols[0, 0], tile_counts[0], tile_set, own, far)
    parts = exchange(parts, FAN_AXES)
    sums = pl.pallas_call(
        collect_kernel,
        out_shape=jax.ShapeDtypeStruct((ZLO, OWN, SUB, LANE), jnp.float32),
        in_specs=[SMEM] * 6 + [VMEM],
        out_specs=VMEM,
        name="collect",
    )(*where, parts)
    sums = exchange(sums.reshape(ZLO * OWN, SUB, LANE), OUT_AXES)
    total = jnp.sum(sums.reshape(ZLO * ZHI, vecs, LANE), axis=0)
    return total[None]


def solution(mesh):
    fine = Mesh(mesh.devices.reshape(ZLO, X, ZHI, Y, CORE), ("zlo", "x", "zhi", "y", "core"))
    return jax.shard_map(
        on_device,
        mesh=fine,
        in_specs=(
            P(OWN_AXES, None, None),
            P(GRP_AXES, OWN_AXES, None, None, None),
            P(GRP_AXES, OWN_AXES, None),
            P(GRP_AXES, OWN_AXES, None),
            P(GRP_AXES, OWN_AXES),
            P(GRP_AXES, None),
        ),
        out_specs=P(OWN_AXES, None, GRP_AXES),
        check_vma=False,
    )
```

profile of v0, /device:TPU:1, one launch (start us, length us, event | category | flops | bytes accessed | tf_op | source)
XLA Modules:
  0.0 127.7 jit_solution(10632934164140131543)
XLA Ops:
  0.0 1.8 %pieces.1 = f32[16,4,8,128]{3,2,1,0:T(8,128)} custom-call(s32[1]{0:T(128)} %bitcast.x_ref, f32[64,2048]{1,0:T(8,128)} %bitcast.14), custom_call_target="tpu_custom_call" | custom-call | tf_op jit(solution)/shard_map/pieces/pallas_call | solution.py:163
  1.8 12.6 %all-to-all-start = ((f32[16,4,8,128]{3,2,1,0:T(8,128)}), f32[16,4,8,128]{3,2,1,0:T(8,128)S(1)}, u32[]{:S(2)}, u32[]{:S(2)}) async-start(f32[16,4,8,128]{3,2,1,0:T(8,128)} %pieces.1), calls=%async_computation | async-start | bytes 524288 | tf_op jit(solution)/shard_map/all_to_all | solution.py:148
  14.4 1.2 collective-permute-start.2
  15.6 2.4 %collective-permute-start.1 = (s32[1,3]{1,0:T(1,128)}, s32[1,3]{1,0:T(1,128)S(1)}, u32[]{:S(2)}, u32[]{:S(2)}) collective-permute-start(s32[1,3]{1,0:T(1,128)} %m0.3), channel_id=1, source_target_pairs={{0,32},{16,48},{32,0},{48,16},{1,33},{17,49},{33,1},{49,17},{2,34}... | collective-permute-start | bytes 44 | tf_op jit(solution)/shard_map/ppermute | solution.py:158
  18.0 1.2 collective-permute-start
  19.2 0.0 collective-permute-done.2.m3
  19.2 0.0 copy-start.2
  19.2 0.4 collective-permute-done.1.m2
  19.6 0.0 copy-start.3
  19.6 1.2 collective-permute-done.m1
  20.9 0.0 copy-start.4
  20.9 4.6 %all-to-all-done.pieces_ref = f32[16,4,8,128]{3,2,1,0:T(8,128)S(1)} async-done(((f32[16,4,8,128]{3,2,1,0:T(8,128)}), f32[16,4,8,128]{3,2,1,0:T(8,128)S(1)}, u32[]{:S(2)}, u32[]{:S(2)}) %all-to-all-start) | async-done | bytes 262176 | tf_op jit(solution)/shard_map/all_to_all | solution.py:148
  25.5 0.0 copy-start.1
  25.5 0.0 copy-done.2
  25.5 0.0 copy-done.3
  25.5 0.0 copy-done.4
  25.5 0.7 copy-done.1
  26.2 2.2 %route.1 = f32[32,3,4,8,128]{4,3,2,1,0:T(8,128)} custom-call(s32[1]{0:T(128)} %bitcast.x_ref, s32[1]{0:T(128)} %bitcast.1.zhi_ref, s32[1,3]{1,0:T(1,128)} %m0.3, s32[1,3]{1,0:T(1,128)} %copy-done.4, s32[1,3]{1,0:T(1,128)} %copy-done.3, s32[1,3]{1,0:T(1,128)} %copy-done.2, f32[16,4,8,128]{3,2,1,0:T(8,128)} %copy-done.1), custom_call_target="tpu_custom_call" | custom-call | tf_op jit(solution)/shard_map/route/pallas_call | solution.py:171
  28.4 5.8 %all-to-all-start.1 = ((f32[32,3,4,8,128]{4,3,2,1,0:T(8,128)}), f32[32,3,4,8,128]{4,3,2,1,0:T(8,128)S(1)}, u32[]{:S(2)}, u32[]{:S(2)}) async-start(f32[32,3,4,8,128]{4,3,2,1,0:T(8,128)} %route.1), calls=%async_computation.1 | async-start | bytes 3145728 | tf_op jit(solution)/shard_map/all_to_all | solution.py:148
  34.9 22.0 %all-to-all-done.1.far_ref = f32[32,3,4,8,128]{4,3,2,1,0:T(8,128)S(1)} async-done(((f32[32,3,4,8,128]{4,3,2,1,0:T(8,128)}), f32[32,3,4,8,128]{4,3,2,1,0:T(8,128)S(1)}, u32[]{:S(2)}, u32[]{:S(2)}) %all-to-all-start.1) | async-done | bytes 1572896 | tf_op jit(solution)/shard_map/all_to_all | solution.py:148
  56.9 0.0 copy-start
  56.9 1.1 copy-done
  58.1 13.7 %products.1 = f32[32,4,4,8,128]{4,3,2,1,0:T(8,128)} custom-call(s32[128]{0:T(128)} %bitcast.18, s32[128]{0:T(128)} %bitcast.19, s32[1]{0:T(128)} %bitcast.12.count, f32[128,128,128]{2,1,0:T(8,128)} %bitcast.13, f32[64,2048]{1,0:T(8,128)} %bitcast.15, f32[32,3,4,8,128]{4,3,2,1,0:T(8,128)} %copy-done), custom_call_target="tpu_custom_call" | custom-call | tf_op jit(solution)/shard_map/products/pallas_call | solution.py:179
  71.8 31.8 %all_to_all.20.parts_ref = f32[32,4,4,8,128]{4,3,2,1,0:T(8,128)} all-to-all(f32[32,4,4,8,128]{4,3,2,1,0:T(8,128)} %products.1), channel_id=1, replica_groups=mesh['zlo'=4,'x'=4,'zhi'=2,'y'=4,'core'=2] {'x','y','core'}, dimensions={0} | all-to-all | bytes 4194304 | tf_op jit(solution)/shard_map/all_to_all | solution.py:148
  103.6 2.8 %collect.1 = f32[4,16,8,128]{3,2,1,0:T(8,128)} custom-call(s32[1]{0:T(128)} %bitcast.x_ref, s32[1]{0:T(128)} %bitcast.1.zhi_ref, s32[1,3]{1,0:T(1,128)} %m0.3, s32[1,3]{1,0:T(1,128)} %copy-done.4, s32[1,3]{1,0:T(1,128)} %copy-done.3, s32[1,3]{1,0:T(1,128)} %copy-done.2, f32[32,4,4,8,128]{4,3,2,1,0:T(8,128)} %all_to_all.20.parts_ref), custom_call_target="tpu_custom_call" | custom-call | tf_op jit(solution)/shard_map/collect/pallas_call | solution.py:192
  106.4 20.6 %all_to_all.21 = f32[64,8,128]{2,1,0:T(8,128)S(1)} all-to-all(f32[64,8,128]{2,1,0:T(8,128)} %bitcast.16), channel_id=1, replica_groups=mesh['zlo'=4,'x'=4,'zhi'=2,'y'=4,'core'=2] {'zlo','zhi','y','core'}, dimensions={0} | all-to-all | bytes 524288 | tf_op jit(solution)/shard_map/all_to_all | solution.py:148
  127.0 0.6 bitcast_reduce_fusion
Async XLA Ops:
  1.8 23.7 %all-to-all-start = ((f32[16,4,8,128]{3,2,1,0:T(8,128)}), f32[16,4,8,128]{3,2,1,0:T(8,128)S(1)}, u32[]{:S(2)}, u32[]{:S(2)}) async-start(f32[16,4,8,128]{3,2,1,0:T(8,128)} %pieces.1), calls=%async_computation | async-start | bytes 524288 | tf_op jit(solution)/shard_map/all_to_all | solution.py:148
  14.4 4.8 %collective-permute-start.2 = (s32[1,3]{1,0:T(1,128)}, s32[1,3]{1,0:T(1,128)S(1)}, u32[]{:S(2)}, u32[]{:S(2)}) collective-permute-start(s32[1,3]{1,0:T(1,128)} %m0.3), channel_id=1, source_target_pairs={{0,16},{16,32},{32,48},{48,0},{1,17},{17,33},{33,49},{49,1},{2,18}... | collective-permute-start | bytes 44 | tf_op jit(solution)/shard_map/ppermute | solution.py:158
  15.6 4.1 %collective-permute-start.1 = (s32[1,3]{1,0:T(1,128)}, s32[1,3]{1,0:T(1,128)S(1)}, u32[]{:S(2)}, u32[]{:S(2)}) collective-permute-start(s32[1,3]{1,0:T(1,128)} %m0.3), channel_id=1, source_target_pairs={{0,32},{16,48},{32,0},{48,16},{1,33},{17,49},{33,1},{49,17},{2,34}... | collective-permute-start | bytes 44 | tf_op jit(solution)/shard_map/ppermute | solution.py:158
  18.0 2.8 %collective-permute-start = (s32[1,3]{1,0:T(1,128)}, s32[1,3]{1,0:T(1,128)S(1)}, u32[]{:S(2)}, u32[]{:S(2)}) collective-permute-start(s32[1,3]{1,0:T(1,128)} %m0.3), channel_id=1, source_target_pairs={{0,48},{16,0},{32,16},{48,32},{1,49},{17,1},{33,17},{49,33},{2,50}... | collective-permute-start | bytes 44 | tf_op jit(solution)/shard_map/ppermute | solution.py:158
  19.2 6.3 %copy-start.2 = (s32[1,3]{1,0:T(1,128)}, s32[1,3]{1,0:T(1,128)S(1)}, u32[]{:S(2)}) copy-start(s32[1,3]{1,0:T(1,128)S(1)} %collective-permute-done.2.m3) | copy-start | bytes 40
  19.6 5.9 %copy-start.3 = (s32[1,3]{1,0:T(1,128)}, s32[1,3]{1,0:T(1,128)S(1)}, u32[]{:S(2)}) copy-start(s32[1,3]{1,0:T(1,128)S(1)} %collective-permute-done.1.m2) | copy-start | bytes 40
  20.9 4.6 %copy-start.4 = (s32[1,3]{1,0:T(1,128)}, s32[1,3]{1,0:T(1,128)S(1)}, u32[]{:S(2)}) copy-start(s32[1,3]{1,0:T(1,128)S(1)} %collective-permute-done.m1) | copy-start | bytes 40
  25.5 0.7 copy-start.1
  28.4 28.5 %all-to-all-start.1 = ((f32[32,3,4,8,128]{4,3,2,1,0:T(8,128)}), f32[32,3,4,8,128]{4,3,2,1,0:T(8,128)S(1)}, u32[]{:S(2)}, u32[]{:S(2)}) async-start(f32[32,3,4,8,128]{4,3,2,1,0:T(8,128)} %route.1), calls=%async_computation.1 | async-start | bytes 3145728 | tf_op jit(solution)/shard_map/all_to_all | solution.py:148
  56.9 1.1 copy-start
where the time goes:
time: 127 us; the launch traced here: 128 us
  blocking collectives  52.4 us (41%)
  waiting for transfers between devices  28.3 us (22%)
  starting transfers between devices  23.3 us (18%)
  Pallas kernels  20.5 us (16%)
  local copies, waits for them, and re-layouts  1.84 us (1%)
    all_to_all x2, blocking collectives, exchange(): return lax.all_to_all(value, axes, 0, 0, tiled=False)  52.4 us
    all_to_all x2, waiting for transfers between devices, exchange(): return lax.all_to_all(value, axes, 0, 0, tiled=False)  26.6 us
    all_to_all x2, starting transfers between devices, exchange(): return lax.all_to_all(value, axes, 0, 0, tiled=False)  18.5 us
    pallas_call x1, Pallas kernels, on_device(): pl.pallas_call(products_kernel, out_shape=jax.ShapeDtypeStruct((FAN, REGI...  13.7 us
    ppermute x3, starting transfers between devices, on_device(): lax.ppermute(matchings, 'x', [(i, (i - step) % X) for i in range(X)])  4.81 us
    pallas_call x1, Pallas kernels, on_device(): pl.pallas_call(collect_kernel, out_shape=jax.ShapeDtypeStruct((ZLO, OWN,...  2.81 us
  transfers between devices with their start and end apart: 5, of which 4 were waited for; matrix products, arithmetic and copies ran while one was open for 0% of the time, Pallas kernels for 0%

commit v1 on v0

v1 whole, which is shorter than its diff:
```python
import jax
import jax.numpy as jnp
from jax import lax
from jax.experimental import pallas as pl
from jax.experimental.pallas import tpu as pltpu
from jax.sharding import Mesh, PartitionSpec as P

ZLO, X, ZHI, Y, CORE = 4, 4, 2, 4, 2
YC = Y * CORE
OWN = ZHI * YC
FAN = X * YC
GRP_AXES = ("zlo", "x")
OWN_AXES = ("zhi", "y", "core")
FAN_AXES = ("x", "y", "core")
OUT_AXES = ("zlo", "zhi", "y", "core")

REGIONS = 4
SUB = 8
LANE = 128
CHUNK = 16
GROUP = 8
SMALL = 8 << 20
LARGE = 56 << 20

VMEM = pl.BlockSpec(memory_space=pltpu.VMEM)
SMEM = pl.BlockSpec(memory_space=pltpu.SMEM)
HBM = pl.BlockSpec(memory_space=pltpu.HBM)

BY_COLS = (((1,), (0,)), ((), ()))
BY_ROWS = (((1,), (1,)), ((), ()))


def halves(value):
    high = value.astype(jnp.bfloat16)
    return high, (value - high.astype(jnp.float32)).astype(jnp.bfloat16)


def product(pair, high, low, dims):
    both = jnp.concatenate([high, low], axis=1 if dims is BY_COLS else 0)
    wide = lax.dot_general(pair, both, dims, preferred_element_type=jnp.float32)
    count = pair.shape[0] // 2
    return wide[:count, :LANE] + wide[count:, :LANE] + wide[:count, LANE:]


def pieces_kernel(x_ref, own_ref, out_ref):
    x = x_ref[0]
    for zlo in range(ZLO):
        start = pl.multiple_of((zlo * X + x) * LANE, LANE)
        for part in range(YC):
            block = own_ref[part * SUB : (part + 1) * SUB, pl.ds(start, LANE)]
            for zhi in range(ZHI):
                out_ref[zhi * YC + part, zlo] = block


def route_kernel(x_ref, zhi_ref, m0, m1, m2, m3, pieces_ref, out_ref):
    x = x_ref[0]
    first = zhi_ref[0] * YC
    for step, masks in enumerate((m0, m1, m2, m3)):
        base = lax.rem(x + step, X) * YC
        for slot in range(REGIONS - 1):
            mask = masks[0, slot]
            for part in range(YC):
                out_ref[base + part, slot] = pieces_ref[(first + part) ^ mask]


def collect_kernel(x_ref, zhi_ref, m0, m1, m2, m3, parts_ref, out_ref):
    x = x_ref[0]
    first = zhi_ref[0] * YC
    out_ref[...] = jnp.zeros_like(out_ref)
    for step, masks in enumerate((m0, m1, m2, m3)):
        base = lax.rem(x + step, X) * YC
        for slot in range(REGIONS - 1):
            for part in range(YC):
                owner = (first + part) ^ masks[0, slot]
                for zlo in range(ZLO):
                    out_ref[zlo, owner] += parts_ref[base + part, slot, zlo]


def load_table(table, base, blocks, get, vecs):
    for block in range(blocks):
        high, low = halves(get(block))
        table[base + block, :vecs] = high
        table[base + block, vecs:] = low


def fetch(tiles, held, sems):
    copies = [
        pltpu.make_async_copy(
            tiles.at[pl.ds(i * CHUNK, CHUNK)], held.at[pl.ds(i * CHUNK, CHUNK)], sems.at[i]
        )
        for i in range(held.shape[0] // CHUNK)
    ]
    for copy in copies:
        copy.start()
    return copies


def each_group(copies, live, group):
    for i, copy in enumerate(copies):
        copy.wait()
        here = jnp.clip(live - i * CHUNK, 0, CHUNK)
        full = here // GROUP

        def several(step, carry, i=i):
            group(i * CHUNK + step * GROUP, GROUP)
            return carry

        def single(step, carry, i=i):
            group(i * CHUNK + step, 1)
            return carry

        lax.fori_loop(0, full, several, 0)
        lax.fori_loop(full * GROUP, here, single, 0)


def columns_kernel(rows, cols, count, tiles, own_ref, out_ref, self_ref, held, table, sums, sems):
    copies = fetch(tiles, held, sems)
    sums[...] = jnp.zeros_like(sums)
    vecs = own_ref.shape[0]
    blocks = own_ref.shape[1] // LANE
    load_table(table, 0, blocks, lambda b: own_ref[:, b * LANE : (b + 1) * LANE], vecs)

    def group(first, size):
        done = []
        for k in range(size):
            high, low = halves(held[first + k])
            done.append(product(table[rows[first + k]], high, low, BY_COLS))
        for k in range(size):
            col = cols[first + k]
            sums[col] += done[k]

    each_group(copies, count[0], group)
    self_ref[...] = sums[:blocks]
    for slot in range(REGIONS - 1):
        for block in range(blocks):
            zlo, x = divmod(block, X)
            value = sums[(slot + 1) * blocks + block]
            for part in range(YC):
                out_ref[x * YC + part, slot, zlo] = value[part * SUB : (part + 1) * SUB]


def rows_kernel(x_ref, rows, cols, count, tiles, own_ref, far_ref, self_ref, *rest):
    outs, (held, table, sums, sems) = rest[:X], rest[X:]
    copies = fetch(tiles, held, sems)
    sums[...] = self_ref[...]
    vecs = own_ref.shape[0]
    blocks = own_ref.shape[1] // LANE
    load_table(table, 0, blocks, lambda b: own_ref[:, b * LANE : (b + 1) * LANE], vecs)
    for slot in range(REGIONS - 1):

        def far(b, slot=slot):
            return jnp.concatenate(
                [far_ref[b % X * YC + part, slot, b // X] for part in range(YC)], axis=0
            )

        load_table(table, (slot + 1) * blocks, blocks, far, vecs)

    def group(first, size):
        done = []
        for k in range(size):
            high, low = halves(held[first + k])
            done.append(product(table[cols[first + k]], high, low, BY_ROWS))
        for k in range(size):
            row = rows[first + k]
            sums[row] += done[k]

    each_group(copies, count[0], group)
    for step in range(X):
        x = lax.rem(x_ref[0] + step, X)
        for zlo in range(ZLO):
            outs[step][zlo] = sums[zlo * X + x]


def spread_kernel(zlo_ref, a_ref, b_ref, c_ref, d_ref, *outs):
    for step in range(ZLO):
        z = zlo_ref[0] ^ step
        outs[step][...] = (a_ref[z] + b_ref[z]) + (c_ref[z] + d_ref[z])


def exchange(value, axes):
    return lax.all_to_all(value, axes, 0, 0, tiled=False)


def local(kernel, outs, specs, scratch=(), limit=None, cost=None):
    outs = [jax.ShapeDtypeStruct(shape, jnp.float32) for shape in outs]
    return pl.pallas_call(
        kernel,
        out_shape=outs,
        in_specs=specs,
        out_specs=[VMEM] * len(outs),
        scratch_shapes=scratch,
        compiler_params=pltpu.CompilerParams(vmem_limit_bytes=limit),
        cost_estimate=cost,
        name=kernel.__name__,
    )


def on_device(vectors, tiles, tile_rows, tile_cols, tile_counts, matchings):
    own = vectors[0]
    tile_set = tiles[0, 0]
    vecs, rows_own = own.shape
    slots = tile_set.shape[0]
    blocks = rows_own // LANE
    x, zhi, zlo = (
        lax.axis_index(axis).reshape(1).astype(jnp.int32) for axis in ("x", "zhi", "zlo")
    )
    masks = [matchings] + [
        lax.ppermute(matchings, "x", [(i, (i - step) % X) for i in range(X)])
        for step in range(1, X)
    ]
    where = (x, zhi, *masks)
    ids = (tile_rows[0, 0], tile_cols[0, 0], tile_counts[0])
    piece = (ZLO, SUB, LANE)
    half = pl.CostEstimate(
        flops=slots * 6 * vecs * LANE * LANE, bytes_accessed=tile_set.size * 4, transcendentals=0
    )

    def tile_scratch(operand, result):
        return [
            pltpu.VMEM(tile_set.shape, jnp.float32),
            pltpu.VMEM((operand, 2 * vecs, LANE), jnp.bfloat16),
            pltpu.VMEM((result, vecs, LANE), jnp.float32),
            pltpu.SemaphoreType.DMA((slots // CHUNK,)),
        ]

    (pieces,) = local(pieces_kernel, [(OWN, *piece)], [SMEM, VMEM], limit=SMALL)(x, own)
    pieces = exchange(pieces, OWN_AXES)
    parts, mine = local(
        columns_kernel,
        [(FAN, REGIONS - 1, *piece), (blocks, vecs, LANE)],
        [SMEM] * 3 + [HBM, VMEM],
        tile_scratch(blocks, REGIONS * blocks),
        LARGE,
        half,
    )(*ids, tile_set, own)
    parts = exchange(parts, FAN_AXES)
    (wanted,) = local(
        route_kernel, [(FAN, REGIONS - 1, *piece)], [SMEM] * 6 + [VMEM], limit=SMALL
    )(*where, pieces)
    far = exchange(wanted, FAN_AXES)
    (sums,) = local(collect_kernel, [(ZLO, OWN, SUB, LANE)], [SMEM] * 6 + [VMEM], limit=SMALL)(
        *where, parts
    )
    sums = exchange(sums.reshape(ZLO * OWN, SUB, LANE), OUT_AXES)
    rows = local(
        rows_kernel,
        [(ZLO, vecs, LANE)] * X,
        [SMEM] * 4 + [HBM, VMEM, VMEM, VMEM],
        tile_scratch(REGIONS * blocks, blocks),
        LARGE,
        half,
    )(x, *ids, tile_set, own, far, mine)
    rows = [rows[0]] + [
        lax.ppermute(rows[step], "x", [(i, (i + step) % X) for i in range(X)])
        for step in range(1, X)
    ]
    rows = local(spread_kernel, [(vecs, LANE)] * ZLO, [SMEM] + [VMEM] * X, limit=SMALL)(
        zlo, *rows
    )
    rows = [rows[0]] + [
        lax.ppermute(rows[step], "zlo", [(i, i ^ step) for i in range(ZLO)])
        for step in range(1, ZLO)
    ]
    total = jnp.sum(sums.reshape(ZLO * ZHI, vecs, LANE), axis=0)
    for row in rows:
        total = total + row
    return total[None]


def solution(mesh):
    fine = Mesh(mesh.devices.reshape(ZLO, X, ZHI, Y, CORE), ("zlo", "x", "zhi", "y", "core"))
    return jax.shard_map(
        on_device,
        mesh=fine,
        in_specs=(
            P(OWN_AXES, None, None),
            P(GRP_AXES, OWN_AXES, None, None, None),
            P(GRP_AXES, OWN_AXES, None),
            P(GRP_AXES, OWN_AXES, None),
            P(GRP_AXES, OWN_AXES),
            P(GRP_AXES, None),
        ),
        out_specs=P(OWN_AXES, None, GRP_AXES),
        check_vma=False,
    )
```

time: 127 us -> 120 us (0.945)
  the two profiles are of different devices: /device:TPU:1 before, /device:TPU:16 now
where the time goes in v1:
time: 120 us
  starting transfers between devices  51.2 us (43%)
  waiting for transfers between devices  48.5 us (40%)
  Pallas kernels  16.9 us (14%)
  local copies, waits for them, and re-layouts  1.95 us (2%)
    all_to_all x4, starting transfers between devices, exchange(): return lax.all_to_all(value, axes, 0, 0, tiled=False)  34.8 us
    all_to_all x4, waiting for transfers between devices, exchange(): return lax.all_to_all(value, axes, 0, 0, tiled=False)  21.2 us
    ppermute x3, waiting for transfers between devices, on_device(): lax.ppermute(matchings, 'x', [(i, (i - step) % X) for i in range(X)])  15.3 us
    ppermute x3, starting transfers between devices, on_device(): lax.ppermute(rows[step], 'zlo', [(i, i ^ step) for i in range(ZLO)])  6.96 us
    pallas_call x1, Pallas kernels, on_device(): local(rows_kernel, [(ZLO, vecs, LANE)] * X, [SMEM] * 4 + [HBM, VMEM, VMEM...  6.48 us
    ppermute x3, waiting for transfers between devices, on_device(): lax.ppermute(rows[step], 'x', [(i, (i + step) % X) for i in range(X)])  6.35 us
    pallas_call x1, Pallas kernels, on_device(): local(columns_kernel, [(FAN, REGIONS - 1, *piece), (blocks, vecs, LANE)],...  6.22 us
    ppermute x3, starting transfers between devices, on_device(): lax.ppermute(matchings, 'x', [(i, (i - step) % X) for i in range(X)])  5.69 us
  transfers between devices with their start and end apart: 13, of which 9 were waited for; matrix products, arithmetic and copies ran while one was open for 0% of the time, Pallas kernels for 14%

profile of v1, /device:TPU:16, one launch (start us, length us, event | category | flops | bytes accessed | tf_op | source)
XLA Modules:
  0.0 120.1 jit_solution(4620333746804356336)
XLA Ops:
  0.0 1.0 copy-done
  1.0 0.7 pieces_kernel.1
  1.8 11.4 %all-to-all-start.2 = ((f32[16,4,8,128]{3,2,1,0:T(8,128)}), f32[16,4,8,128]{3,2,1,0:T(8,128)S(1)}, u32[]{:S(2)}, u32[]{:S(2)}) async-start(f32[16,4,8,128]{3,2,1,0:T(8,128)} %pieces_kernel.1), calls=%async_computation.2 | async-start | bytes 524288 | tf_op jit(solution)/shard_map/all_to_all | solution.py:181
  13.9 6.2 %columns_kernel.1 = (f32[32,3,4,8,128]{4,3,2,1,0:T(8,128)}, f32[16,64,128]{2,1,0:T(8,128)}) custom-call(s32[128]{0:T(128)} %bitcast.22, s32[128]{0:T(128)} %bitcast.24, s32[1]{0:T(128)} %bitcast.14.count, f32[128,128,128]{2,1,0:T(8,128)} %bitcast.19, f32[64,2048]{1,0:T(8,128)} %bitcast.16), custom_call_target="tpu_custom_call" | custom-call | flops 805306368 | bytes 8388608 | tf_op jit(solution)/shard_map/columns_kernel/pallas_call | solution.py:228
  20.1 2.0 %all-to-all-done.2.pieces_ref = f32[16,4,8,128]{3,2,1,0:T(8,128)S(1)} async-done(((f32[16,4,8,128]{3,2,1,0:T(8,128)}), f32[16,4,8,128]{3,2,1,0:T(8,128)S(1)}, u32[]{:S(2)}, u32[]{:S(2)}) %all-to-all-start.2) | async-done | bytes 262176 | tf_op jit(solution)/shard_map/all_to_all | solution.py:181
  22.1 8.3 %all-to-all-start = ((f32[32,3,4,8,128]{4,3,2,1,0:T(8,128)}), f32[32,3,4,8,128]{4,3,2,1,0:T(8,128)S(1)}, u32[]{:S(2)}, u32[]{:S(2)}) async-start(f32[32,3,4,8,128]{4,3,2,1,0:T(8,128)} %get-tuple-element.15), calls=%async_computation | async-start | bytes 3145728 | tf_op jit(solution)/shard_map/all_to_all | solution.py:181
  30.4 1.5 %collective-permute-start.2 = (s32[1,3]{1,0:T(1,128)S(1)}, s32[1,3]{1,0:T(1,128)S(1)}, u32[]{:S(2)}, u32[]{:S(2)}) collective-permute-start(s32[1,3]{1,0:T(1,128)S(1)} %copy-done.2), channel_id=1, source_target_pairs={{0,16},{16,32},{32,48},{48,0},{1,17},{17,33},{33,49},{49,1},{2,18}... | collective-permute-start | bytes 44 | tf_op jit(solution)/shard_map/ppermute | solution.py:208
  31.9 2.7 %collective-permute-start.1 = (s32[1,3]{1,0:T(1,128)S(1)}, s32[1,3]{1,0:T(1,128)S(1)}, u32[]{:S(2)}, u32[]{:S(2)}) collective-permute-start(s32[1,3]{1,0:T(1,128)S(1)} %copy-done.2), channel_id=1, source_target_pairs={{0,32},{16,48},{32,0},{48,16},{1,33},{17,49},{33,1},{49,17},{2,34}... | collective-permute-start | bytes 44 | tf_op jit(solution)/shard_map/ppermute | solution.py:208
  34.6 1.4 %collective-permute-start = (s32[1,3]{1,0:T(1,128)S(1)}, s32[1,3]{1,0:T(1,128)S(1)}, u32[]{:S(2)}, u32[]{:S(2)}) collective-permute-start(s32[1,3]{1,0:T(1,128)S(1)} %copy-done.2), channel_id=1, source_target_pairs={{0,48},{16,0},{32,16},{48,32},{1,49},{17,1},{33,17},{49,33},{2,50}... | collective-permute-start | bytes 44 | tf_op jit(solution)/shard_map/ppermute | solution.py:208
  36.0 14.3 %collective-permute-done.2.m3 = s32[1,3]{1,0:T(1,128)S(1)} collective-permute-done((s32[1,3]{1,0:T(1,128)S(1)}, s32[1,3]{1,0:T(1,128)S(1)}, u32[]{:S(2)}, u32[]{:S(2)}) %collective-permute-start.2) | collective-permute-done | bytes 44 | tf_op jit(solution)/shard_map/ppermute | solution.py:208
  50.4 1.0 collective-permute-done.1.m2
  51.4 1.8 %route_kernel.1 = f32[32,3,4,8,128]{4,3,2,1,0:T(8,128)} custom-call(s32[1]{0:T(128)} %bitcast.x_ref, s32[1]{0:T(128)} %bitcast.1.zhi_ref, s32[1,3]{1,0:T(1,128)S(1)} %copy-done.2, s32[1,3]{1,0:T(1,128)S(1)} %collective-permute-done.m1, s32[1,3]{1,0:T(1,128)S(1)} %collective-permute-done.1.m2, s32[1,3]{1,0:T(1,128)S(1)} %collective-permute-done.2.m3, ...), custom_call_target="tpu_custom_call" | custom-call | tf_op jit(solution)/shard_map/route_kernel/pallas_call | solution.py:237
  53.2 0.0 all-to-all-done.parts_ref
  53.2 5.6 %all-to-all-start.3 = ((f32[32,3,4,8,128]{4,3,2,1,0:T(8,128)}), f32[32,3,4,8,128]{4,3,2,1,0:T(8,128)S(1)}, u32[]{:S(2)}, u32[]{:S(2)}) async-start(f32[32,3,4,8,128]{4,3,2,1,0:T(8,128)} %route_kernel.1), calls=%async_computation.3 | async-start | bytes 3145728 | tf_op jit(solution)/shard_map/all_to_all | solution.py:181
  58.8 1.7 %collect_kernel.1 = f32[4,16,8,128]{3,2,1,0:T(8,128)} custom-call(s32[1]{0:T(128)} %bitcast.x_ref, s32[1]{0:T(128)} %bitcast.1.zhi_ref, s32[1,3]{1,0:T(1,128)S(1)} %copy-done.2, s32[1,3]{1,0:T(1,128)S(1)} %collective-permute-done.m1, s32[1,3]{1,0:T(1,128)S(1)} %collective-permute-done.1.m2, s32[1,3]{1,0:T(1,128)S(1)} %collective-permute-done.2.m3, ...), custom_call_target="tpu_custom_call" | custom-call | tf_op jit(solution)/shard_map/collect_kernel/pallas_call | solution.py:241
  60.5 19.2 %all-to-all-done.3.far_ref = f32[32,3,4,8,128]{4,3,2,1,0:T(8,128)S(1)} async-done(((f32[32,3,4,8,128]{4,3,2,1,0:T(8,128)}), f32[32,3,4,8,128]{4,3,2,1,0:T(8,128)S(1)}, u32[]{:S(2)}, u32[]{:S(2)}) %all-to-all-start.3) | async-done | bytes 1572896 | tf_op jit(solution)/shard_map/all_to_all | solution.py:181
  79.7 9.4 %all-to-all-start.1 = ((f32[64,8,128]{2,1,0:T(8,128)}), f32[64,8,128]{2,1,0:T(8,128)S(1)}, u32[]{:S(2)}, u32[]{:S(2)}) async-start(f32[64,8,128]{2,1,0:T(8,128)} %bitcast.7), calls=%async_computation.1 | async-start | bytes 524288 | tf_op jit(solution)/shard_map/all_to_all | solution.py:181
  89.2 6.5 %rows_kernel.1 = (f32[4,64,128]{2,1,0:T(8,128)}, f32[4,64,128]{2,1,0:T(8,128)}, f32[4,64,128]{2,1,0:T(8,128)}, f32[4,64,128]{2,1,0:T(8,128)}) custom-call(s32[1]{0:T(128)} %bitcast.x_ref, s32[128]{0:T(128)} %bitcast.23, s32[128]{0:T(128)} %bitcast.25, s32[1]{0:T(128)} %bitcast.15.count, f32[128,128,128]{2,1,0:T(8,128)} %bitcast.20, f32[64,2048]{1,0:T(8,128)} %bitcast.17, ...), custom_call_target="tpu_custom_call" | custom-call | flops 805306368 | bytes 8388608 | tf_op jit(solution)/shard_map/rows_kernel/pallas_call | solution.py:245
  95.7 0.3 collective-permute-start.3
  96.0 2.4 %collective-permute-start.4 = (f32[4,64,128]{2,1,0:T(8,128)}, f32[4,64,128]{2,1,0:T(8,128)S(1)}, u32[]{:S(2)}, u32[]{:S(2)}) collective-permute-start(f32[4,64,128]{2,1,0:T(8,128)} %get-tuple-element.19), channel_id=1, source_target_pairs={{0,32},{16,48},{32,0},{48,16},{1,33},{17,49},{33,1},{49,17},{2,34}... | collective-permute-start | bytes 393224 | tf_op jit(solution)/shard_map/ppermute | solution.py:254
  98.3 1.1 collective-permute-start.5
  99.5 2.7 %collective-permute-done.3.b_ref = f32[4,64,128]{2,1,0:T(8,128)S(1)} collective-permute-done((f32[4,64,128]{2,1,0:T(8,128)}, f32[4,64,128]{2,1,0:T(8,128)S(1)}, u32[]{:S(2)}, u32[]{:S(2)}) %collective-permute-start.3) | collective-permute-done | bytes 131104 | tf_op jit(solution)/shard_map/ppermute | solution.py:254
  102.2 3.1 %collective-permute-done.4.c_ref = f32[4,64,128]{2,1,0:T(8,128)S(1)} collective-permute-done((f32[4,64,128]{2,1,0:T(8,128)}, f32[4,64,128]{2,1,0:T(8,128)S(1)}, u32[]{:S(2)}, u32[]{:S(2)}) %collective-permute-start.4) | collective-permute-done | bytes 131104 | tf_op jit(solution)/shard_map/ppermute | solution.py:254
  105.3 0.6 collective-permute-done.5.d_ref
  105.8 0.9 copy-done.1
  106.8 3.2 %collective-permute-start.6 = (f32[64,128]{1,0:T(8,128)S(1)}, f32[64,128]{1,0:T(8,128)S(1)}, u32[]{:S(2)}, u32[]{:S(2)}) collective-permute-start(f32[64,128]{1,0:T(8,128)S(1)} %get-tuple-element.22), channel_id=1, source_target_pairs={{0,64},{64,0},{128,192},{192,128},{1,65},{65,1},{129,193},{193,129... | collective-permute-start | bytes 98312 | tf_op jit(solution)/shard_map/ppermute | solution.py:261
  110.0 3.8 %collective-permute-start.7 = (f32[64,128]{1,0:T(8,128)S(1)}, f32[64,128]{1,0:T(8,128)S(1)}, u32[]{:S(2)}, u32[]{:S(2)}) collective-permute-start(f32[64,128]{1,0:T(8,128)S(1)} %get-tuple-element.23), channel_id=1, source_target_pairs={{0,128},{64,192},{128,0},{192,64},{1,129},{65,193},{129,1},{193,65... | collective-permute-start | bytes 98312 | tf_op jit(solution)/shard_map/ppermute | solution.py:261
  113.7 0.0 collective-permute-start.8
  113.7 0.0 all-to-all-done.1
  113.8 2.0 %collective-permute-done.7 = f32[64,128]{1,0:T(8,128)S(1)} collective-permute-done((f32[64,128]{1,0:T(8,128)S(1)}, f32[64,128]{1,0:T(8,128)S(1)}, u32[]{:S(2)}, u32[]{:S(2)}) %collective-permute-start.7) | collective-permute-done | bytes 32800 | tf_op jit(solution)/shard_map/ppermute | solution.py:261
  115.8 3.7 %collective-permute-done.8 = f32[64,128]{1,0:T(8,128)S(1)} collective-permute-done((f32[64,128]{1,0:T(8,128)S(1)}, f32[64,128]{1,0:T(8,128)S(1)}, u32[]{:S(2)}, u32[]{:S(2)}) %collective-permute-start.8) | collective-permute-done | bytes 32800 | tf_op jit(solution)/shard_map/ppermute | solution.py:261
  119.4 0.6 add_bitcast_fusion
  (10 shorter events, 0.1 us)
Async XLA Ops:
  0.0 1.0 copy-start
  1.8 20.3 %all-to-all-start.2 = ((f32[16,4,8,128]{3,2,1,0:T(8,128)}), f32[16,4,8,128]{3,2,1,0:T(8,128)S(1)}, u32[]{:S(2)}, u32[]{:S(2)}) async-start(f32[16,4,8,128]{3,2,1,0:T(8,128)} %pieces_kernel.1), calls=%async_computation.2 | async-start | bytes 524288 | tf_op jit(solution)/shard_map/all_to_all | solution.py:181
  22.1 8.3 %copy-start.2 = (s32[1,3]{1,0:T(1,128)S(1)}, s32[1,3]{1,0:T(1,128)}, u32[]{:S(2)}) copy-start(s32[1,3]{1,0:T(1,128)} %m0.3) | copy-start | bytes 40
  22.1 31.1 %all-to-all-start = ((f32[32,3,4,8,128]{4,3,2,1,0:T(8,128)}), f32[32,3,4,8,128]{4,3,2,1,0:T(8,128)S(1)}, u32[]{:S(2)}, u32[]{:S(2)}) async-start(f32[32,3,4,8,128]{4,3,2,1,0:T(8,128)} %get-tuple-element.15), calls=%async_computation | async-start | bytes 3145728 | tf_op jit(solution)/shard_map/all_to_all | solution.py:181
  30.4 20.0 %collective-permute-start.2 = (s32[1,3]{1,0:T(1,128)S(1)}, s32[1,3]{1,0:T(1,128)S(1)}, u32[]{:S(2)}, u32[]{:S(2)}) collective-permute-start(s32[1,3]{1,0:T(1,128)S(1)} %copy-done.2), channel_id=1, source_target_pairs={{0,16},{16,32},{32,48},{48,0},{1,17},{17,33},{33,49},{49,1},{2,18}... | collective-permute-start | bytes 44 | tf_op jit(solution)/shard_map/ppermute | solution.py:208
  31.9 19.5 %collective-permute-start.1 = (s32[1,3]{1,0:T(1,128)S(1)}, s32[1,3]{1,0:T(1,128)S(1)}, u32[]{:S(2)}, u32[]{:S(2)}) collective-permute-start(s32[1,3]{1,0:T(1,128)S(1)} %copy-done.2), channel_id=1, source_target_pairs={{0,32},{16,48},{32,0},{48,16},{1,33},{17,49},{33,1},{49,17},{2,34}... | collective-permute-start | bytes 44 | tf_op jit(solution)/shard_map/ppermute | solution.py:208
  34.6 16.7 %collective-permute-start = (s32[1,3]{1,0:T(1,128)S(1)}, s32[1,3]{1,0:T(1,128)S(1)}, u32[]{:S(2)}, u32[]{:S(2)}) collective-permute-start(s32[1,3]{1,0:T(1,128)S(1)} %copy-done.2), channel_id=1, source_target_pairs={{0,48},{16,0},{32,16},{48,32},{1,49},{17,1},{33,17},{49,33},{2,50}... | collective-permute-start | bytes 44 | tf_op jit(solution)/shard_map/ppermute | solution.py:208
  53.2 26.5 %all-to-all-start.3 = ((f32[32,3,4,8,128]{4,3,2,1,0:T(8,128)}), f32[32,3,4,8,128]{4,3,2,1,0:T(8,128)S(1)}, u32[]{:S(2)}, u32[]{:S(2)}) async-start(f32[32,3,4,8,128]{4,3,2,1,0:T(8,128)} %route_kernel.1), calls=%async_computation.3 | async-start | bytes 3145728 | tf_op jit(solution)/shard_map/all_to_all | solution.py:181
  79.7 9.5 %copy-start.3 = (f32[32,3,4,8,128]{4,3,2,1,0:T(8,128)}, f32[32,3,4,8,128]{4,3,2,1,0:T(8,128)S(1)}, u32[]{:S(2)}) copy-start(f32[32,3,4,8,128]{4,3,2,1,0:T(8,128)S(1)} %all-to-all-done.3.far_ref) | copy-start | bytes 4718596
  79.7 34.0 %all-to-all-start.1 = ((f32[64,8,128]{2,1,0:T(8,128)}), f32[64,8,128]{2,1,0:T(8,128)S(1)}, u32[]{:S(2)}, u32[]{:S(2)}) async-start(f32[64,8,128]{2,1,0:T(8,128)} %bitcast.7), calls=%async_computation.1 | async-start | bytes 524288 | tf_op jit(solution)/shard_map/all_to_all | solution.py:181
  95.7 6.5 %collective-permute-start.3 = (f32[4,64,128]{2,1,0:T(8,128)}, f32[4,64,128]{2,1,0:T(8,128)S(1)}, u32[]{:S(2)}, u32[]{:S(2)}) collective-permute-start(f32[4,64,128]{2,1,0:T(8,128)} %get-tuple-element.18), channel_id=1, source_target_pairs={{0,16},{16,32},{32,48},{48,0},{1,17},{17,33},{33,49},{49,1},{2,18}... | collective-permute-start | bytes 393224 | tf_op jit(solution)/shard_map/ppermute | solution.py:254
  96.0 9.3 %collective-permute-start.4 = (f32[4,64,128]{2,1,0:T(8,128)}, f32[4,64,128]{2,1,0:T(8,128)S(1)}, u32[]{:S(2)}, u32[]{:S(2)}) collective-permute-start(f32[4,64,128]{2,1,0:T(8,128)} %get-tuple-element.19), channel_id=1, source_target_pairs={{0,32},{16,48},{32,0},{48,16},{1,33},{17,49},{33,1},{49,17},{2,34}... | collective-permute-start | bytes 393224 | tf_op jit(solution)/shard_map/ppermute | solution.py:254
  98.3 7.5 %collective-permute-start.5 = (f32[4,64,128]{2,1,0:T(8,128)}, f32[4,64,128]{2,1,0:T(8,128)S(1)}, u32[]{:S(2)}, u32[]{:S(2)}) collective-permute-start(f32[4,64,128]{2,1,0:T(8,128)} %get-tuple-element.20), channel_id=1, source_target_pairs={{0,48},{16,0},{32,16},{48,32},{1,49},{17,1},{33,17},{49,33},{2,50}... | collective-permute-start | bytes 393224 | tf_op jit(solution)/shard_map/ppermute | solution.py:254
  105.8 0.9 copy-start.1
  106.8 7.0 %collective-permute-start.6 = (f32[64,128]{1,0:T(8,128)S(1)}, f32[64,128]{1,0:T(8,128)S(1)}, u32[]{:S(2)}, u32[]{:S(2)}) collective-permute-start(f32[64,128]{1,0:T(8,128)S(1)} %get-tuple-element.22), channel_id=1, source_target_pairs={{0,64},{64,0},{128,192},{192,128},{1,65},{65,1},{129,193},{193,129... | collective-permute-start | bytes 98312 | tf_op jit(solution)/shard_map/ppermute | solution.py:261
  110.0 5.8 %collective-permute-start.7 = (f32[64,128]{1,0:T(8,128)S(1)}, f32[64,128]{1,0:T(8,128)S(1)}, u32[]{:S(2)}, u32[]{:S(2)}) collective-permute-start(f32[64,128]{1,0:T(8,128)S(1)} %get-tuple-element.23), channel_id=1, source_target_pairs={{0,128},{64,192},{128,0},{192,64},{1,129},{65,193},{129,1},{193,65... | collective-permute-start | bytes 98312 | tf_op jit(solution)/shard_map/ppermute | solution.py:261
  113.7 5.7 %collective-permute-start.8 = (f32[64,128]{1,0:T(8,128)S(1)}, f32[64,128]{1,0:T(8,128)S(1)}, u32[]{:S(2)}, u32[]{:S(2)}) collective-permute-start(f32[64,128]{1,0:T(8,128)S(1)} %get-tuple-element.24), channel_id=1, source_target_pairs={{0,192},{64,128},{128,64},{192,0},{1,193},{65,129},{129,65},{193,1... | collective-permute-start | bytes 98312 | tf_op jit(solution)/shard_map/ppermute | solution.py:261

commit v2 on v1

--- a/solution.py
+++ b/solution.py
@@ -12,7 +12,8 @@
 GRP_AXES = ("zlo", "x")
 OWN_AXES = ("zhi", "y", "core")
 FAN_AXES = ("x", "y", "core")
-OUT_AXES = ("zlo", "zhi", "y", "core")
+YC_AXES = ("y", "core")
+
 
 REGIONS = 4
 SUB = 8
@@ -42,38 +43,62 @@
     return wide[:count, :LANE] + wide[count:, :LANE] + wide[:count, LANE:]
 
 
-def pieces_kernel(x_ref, own_ref, out_ref):
-    x = x_ref[0]
-    for zlo in range(ZLO):
-        start = pl.multiple_of((zlo * X + x) * LANE, LANE)
-        for part in range(YC):
-            block = own_ref[part * SUB : (part + 1) * SUB, pl.ds(start, LANE)]
-            for zhi in range(ZHI):
-                out_ref[zhi * YC + part, zlo] = block
-
-
-def route_kernel(x_ref, zhi_ref, m0, m1, m2, m3, pieces_ref, out_ref):
-    x = x_ref[0]
-    first = zhi_ref[0] * YC
+def pieces_kernel(x_ref, yc_ref, own_ref, *outs):
+    for step in range(YC):
+        row = pl.multiple_of((yc_ref[0] ^ step) * SUB, SUB)
+        for zlo in range(ZLO):
+            col = pl.multiple_of((zlo * X + x_ref[0]) * LANE, LANE)
+            outs[step][zlo] = own_ref[pl.ds(row, SUB), pl.ds(col, LANE)]
+
+
+def gather_kernel(*refs):
+    for step in range(YC):
+        refs[YC][step] = refs[step][...]
+
+
+def route_kernel(x_ref, yc_ref, m0, m1, m2, m3, near_ref, other_ref, out_ref, held):
+    held[:YC] = near_ref[...]
+    held[YC:] = other_ref[...]
     for step, masks in enumerate((m0, m1, m2, m3)):
-        base = lax.rem(x + step, X) * YC
+        base = lax.rem(x_ref[0] + step, X) * YC
         for slot in range(REGIONS - 1):
             mask = masks[0, slot]
             for part in range(YC):
-                out_ref[base + part, slot] = pieces_ref[(first + part) ^ mask]
-
-
-def collect_kernel(x_ref, zhi_ref, m0, m1, m2, m3, parts_ref, out_ref):
-    x = x_ref[0]
-    first = zhi_ref[0] * YC
-    out_ref[...] = jnp.zeros_like(out_ref)
+                out_ref[base + part, slot] = held[(part ^ yc_ref[0]) ^ mask]
+
+
+def collect_kernel(x_ref, yc_ref, zlo_ref, m0, m1, m2, m3, parts_ref, near_ref, other_ref, sums):
+    sums[...] = jnp.zeros_like(sums)
     for step, masks in enumerate((m0, m1, m2, m3)):
-        base = lax.rem(x + step, X) * YC
+        base = lax.rem(x_ref[0] + step, X) * YC
         for slot in range(REGIONS - 1):
+            mask = masks[0, slot]
             for part in range(YC):
-                owner = (first + part) ^ masks[0, slot]
+                owner = (part ^ yc_ref[0]) ^ mask
                 for zlo in range(ZLO):
-                    out_ref[zlo, owner] += parts_ref[base + part, slot, zlo]
+                    sums[zlo, owner] += parts_ref[base + part, slot, zlo]
+    for step in range(ZLO):
+        zlo = zlo_ref[0] ^ step
+        near_ref[step] = sums[zlo, :YC]
+        other_ref[step] = sums[zlo, YC:]
+
+
+def add_zhi_kernel(a_ref, b_ref, *outs):
+    for step in range(ZLO):
+        outs[step][...] = a_ref[step] + b_ref[step]
+
+
+def add_zlo_kernel(a_ref, b_ref, c_ref, d_ref, *outs):
+    for step in range(YC):
+        outs[step][...] = (a_ref[step] + b_ref[step]) + (c_ref[step] + d_ref[step])
+
+
+def final_kernel(yc_ref, *refs):
+    parts, rows, out_ref = refs[:YC], refs[YC : YC + ZLO], refs[YC + ZLO]
+    for step in range(YC):
+        at = pl.ds(pl.multiple_of((yc_ref[0] ^ step) * SUB, SUB), SUB)
+        own = (rows[0][at] + rows[1][at]) + (rows[2][at] + rows[3][at])
+        out_ref[at] = own + parts[step][...]
 
 
 def load_table(table, base, blocks, get, vecs):
@@ -191,8 +216,14 @@
         scratch_shapes=scratch,
         compiler_params=pltpu.CompilerParams(vmem_limit_bytes=limit),
         cost_estimate=cost,
-        name=kernel.__name__,
-    )
+    )
+
+
+def swaps(arrays, axes, count):
+    return [arrays[0]] + [
+        lax.ppermute(arrays[step], axes, [(i, i ^ step) for i in range(count)])
+        for step in range(1, count)
+    ]
 
 
 def on_device(vectors, tiles, tile_rows, tile_cols, tile_counts, matchings):
@@ -201,14 +232,9 @@
     vecs, rows_own = own.shape
     slots = tile_set.shape[0]
     blocks = rows_own // LANE
-    x, zhi, zlo = (
-        lax.axis_index(axis).reshape(1).astype(jnp.int32) for axis in ("x", "zhi", "zlo")
-    )
-    masks = [matchings] + [
-        lax.ppermute(matchings, "x", [(i, (i - step) % X) for i in range(X)])
-        for step in range(1, X)
-    ]
-    where = (x, zhi, *masks)
+    x, zlo, yc = (
+        lax.axis_index(axes).reshape(1).astype(jnp.int32) for axes in ("x", "zlo", YC_AXES)
+    )
     ids = (tile_rows[0, 0], tile_cols[0, 0], tile_counts[0])
     piece = (ZLO, SUB, LANE)
     half = pl.CostEstimate(
@@ -223,8 +249,12 @@
             pltpu.SemaphoreType.DMA((slots // CHUNK,)),
         ]
 
-    (pieces,) = local(pieces_kernel, [(OWN, *piece)], [SMEM, VMEM], limit=SMALL)(x, own)
-    pieces = exchange(pieces, OWN_AXES)
+    pieces = local(pieces_kernel, [piece] * YC, [SMEM] * 2 + [VMEM], limit=SMALL)(x, yc, own)
+    pieces = swaps(pieces, YC_AXES, YC)
+    masks = [matchings] + [
+        lax.ppermute(matchings, "x", [(i, (i - step) % X) for i in range(X)])
+        for step in range(1, X)
+    ]
     parts, mine = local(
         columns_kernel,
         [(FAN, REGIONS - 1, *piece), (blocks, vecs, LANE)],
@@ -233,15 +263,33 @@
         LARGE,
         half,
     )(*ids, tile_set, own)
+    (near,) = local(gather_kernel, [(YC, *piece)], [VMEM] * YC, limit=SMALL)(*pieces)
+    parts, near = lax.optimization_barrier((parts, near))
+    other = lax.ppermute(near, "zhi", [(0, 1), (1, 0)])
     parts = exchange(parts, FAN_AXES)
     (wanted,) = local(
-        route_kernel, [(FAN, REGIONS - 1, *piece)], [SMEM] * 6 + [VMEM], limit=SMALL
-    )(*where, pieces)
+        route_kernel,
+        [(FAN, REGIONS - 1, *piece)],
+        [SMEM] * 6 + [VMEM] * 2,
+        [pltpu.VMEM((OWN, *piece), jnp.float32)],
+        SMALL,
+    )(x, yc, *masks, near, other)
+    parts, wanted = lax.optimization_barrier((parts, wanted))
     far = exchange(wanted, FAN_AXES)
-    (sums,) = local(collect_kernel, [(ZLO, OWN, SUB, LANE)], [SMEM] * 6 + [VMEM], limit=SMALL)(
-        *where, parts
-    )
-    sums = exchange(sums.reshape(ZLO * OWN, SUB, LANE), OUT_AXES)
+    spread = (ZLO, YC, SUB, LANE)
+    near, other = local(
+        collect_kernel,
+        [spread] * 2,
+        [SMEM] * 7 + [VMEM],
+        [pltpu.VMEM((ZLO, OWN, SUB, LANE), jnp.float32)],
+        SMALL,
+    )(x, yc, zlo, *masks, parts)
+    other = lax.ppermute(other, "zhi", [(0, 1), (1, 0)])
+    parts = local(add_zhi_kernel, [spread[1:]] * ZLO, [VMEM] * 2, limit=SMALL)(near, other)
+    parts = swaps(parts, "zlo", ZLO)
+    parts = local(add_zlo_kernel, [spread[2:]] * YC, [VMEM] * ZLO, limit=SMALL)(*parts)
+    far, *parts = lax.optimization_barrier((far, *parts))
+    parts = swaps(parts, YC_AXES, YC)
     rows = local(
         rows_kernel,
         [(ZLO, vecs, LANE)] * X,
@@ -257,13 +305,10 @@
     rows = local(spread_kernel, [(vecs, LANE)] * ZLO, [SMEM] + [VMEM] * X, limit=SMALL)(
         zlo, *rows
     )
-    rows = [rows[0]] + [
-        lax.ppermute(rows[step], "zlo", [(i, i ^ step) for i in range(ZLO)])
-        for step in range(1, ZLO)
-    ]
-    total = jnp.sum(sums.reshape(ZLO * ZHI, vecs, LANE), axis=0)
-    for row in rows:
-        total = total + row
+    rows = swaps(rows, "zlo", ZLO)
+    (total,) = local(final_kernel, [(vecs, LANE)], [SMEM] + [VMEM] * (YC + ZLO), limit=SMALL)(
+        yc, *parts, *rows
+    )
     return total[None]
 
 

time: 120 us -> 120 us (level)
  the two profiles are of different devices: /device:TPU:16 before, /device:TPU:1 now
where the time goes in v2:
time: 120 us; the launch traced here: 119 us
  starting transfers between devices  75 us (62%)
  waiting for transfers between devices  24.1 us (20%)
  Pallas kernels  16.3 us (14%)
  local copies, waits for them, and re-layouts  3.12 us (3%)
    ppermute x20, starting transfers between devices, swaps(): lax.ppermute(arrays[step], axes, [(i, i ^ step) for i in range(count)])  38.2 us
    all_to_all x2, starting transfers between devices, exchange(): return lax.all_to_all(value, axes, 0, 0, tiled=False)  11 us
    ppermute x20, waiting for transfers between devices, swaps(): lax.ppermute(arrays[step], axes, [(i, i ^ step) for i in range(count)])  9.59 us
    ppermute x1, starting transfers between devices, on_device(): other = lax.ppermute(near, 'zhi', [(0, 1), (1, 0)])  8 us
    ppermute x1, starting transfers between devices, on_device(): other = lax.ppermute(other, 'zhi', [(0, 1), (1, 0)])  8 us
    ppermute x3, waiting for transfers between devices, on_device(): lax.ppermute(matchings, 'x', [(i, (i - step) % X) for i in range(X)])  7.6 us
    pallas_call x1, Pallas kernels, on_device(): local(rows_kernel, [(ZLO, vecs, LANE)] * X, [SMEM] * 4 + [HBM, VMEM, VMEM...  6.5 us
    pallas_call x1, Pallas kernels, on_device(): local(columns_kernel, [(FAN, REGIONS - 1, *piece), (blocks, vecs, LANE)],...  6.22 us
  transfers between devices with their start and end apart: 30, of which 12 were waited for; matrix products, arithmetic and copies ran while one was open for 0% of the time, Pallas kernels for 8%

profile of v2, /device:TPU:1, one launch (start us, length us, event | category | flops | bytes accessed | tf_op | source)
XLA Modules:
  0.0 119.5 jit_solution(5030996582895337943)
XLA Ops:
  1.1 3.3 %collective-permute-start = (f32[4,8,128]{2,1,0:T(8,128)S(1)}, f32[4,8,128]{2,1,0:T(8,128)S(1)}, u32[]{:S(2)}, u32[]{:S(2)}) collective-permute-start(f32[4,8,128]{2,1,0:T(8,128)S(1)} %get-tuple-element.52), channel_id=1, source_target_pairs={{0,1},{1,0},{2,3},{3,2},{4,5},{5,4},{6,7},{7,6},{8,9},{9,8},{10,11... | collective-permute-start | bytes 49160 | tf_op jit(solution)/shard_map/ppermute | solution.py:224
  4.4 1.7 %collective-permute-start.2 = (f32[4,8,128]{2,1,0:T(8,128)S(1)}, f32[4,8,128]{2,1,0:T(8,128)S(1)}, u32[]{:S(2)}, u32[]{:S(2)}) collective-permute-start(f32[4,8,128]{2,1,0:T(8,128)S(1)} %get-tuple-element.54), channel_id=1, source_target_pairs={{0,3},{1,2},{2,1},{3,0},{4,7},{5,6},{6,5},{7,4},{8,11},{9,10},{10,... | collective-permute-start | bytes 49160 | tf_op jit(solution)/shard_map/ppermute | solution.py:224
  6.1 1.2 %collective-permute-start.3 = (f32[4,8,128]{2,1,0:T(8,128)S(1)}, f32[4,8,128]{2,1,0:T(8,128)S(1)}, u32[]{:S(2)}, u32[]{:S(2)}) collective-permute-start(f32[4,8,128]{2,1,0:T(8,128)S(1)} %get-tuple-element.55), channel_id=1, source_target_pairs={{0,4},{1,5},{2,6},{3,7},{4,0},{5,1},{6,2},{7,3},{8,12},{9,13},{10,... | collective-permute-start | bytes 49160 | tf_op jit(solution)/shard_map/ppermute | solution.py:224
  7.3 2.1 %collective-permute-start.4 = (f32[4,8,128]{2,1,0:T(8,128)S(1)}, f32[4,8,128]{2,1,0:T(8,128)S(1)}, u32[]{:S(2)}, u32[]{:S(2)}) collective-permute-start(f32[4,8,128]{2,1,0:T(8,128)S(1)} %get-tuple-element.56), channel_id=1, source_target_pairs={{0,5},{1,4},{2,7},{3,6},{4,1},{5,0},{6,3},{7,2},{8,13},{9,12},{10,... | collective-permute-start | bytes 49160 | tf_op jit(solution)/shard_map/ppermute | solution.py:224
  11.1 1.9 %collective-permute-start.6 = (f32[4,8,128]{2,1,0:T(8,128)S(1)}, f32[4,8,128]{2,1,0:T(8,128)S(1)}, u32[]{:S(2)}, u32[]{:S(2)}) collective-permute-start(f32[4,8,128]{2,1,0:T(8,128)S(1)} %get-tuple-element.58), channel_id=1, source_target_pairs={{0,7},{1,6},{2,5},{3,4},{4,3},{5,2},{6,1},{7,0},{8,15},{9,14},{10,... | collective-permute-start | bytes 49160 | tf_op jit(solution)/shard_map/ppermute | solution.py:224
  13.1 6.2 %shard_map.64 = (f32[32,3,4,8,128]{4,3,2,1,0:T(8,128)}, f32[16,64,128]{2,1,0:T(8,128)}) custom-call(s32[128]{0:T(128)} %bitcast.16, s32[128]{0:T(128)} %bitcast.18, s32[1]{0:T(128)} %bitcast.9.count, f32[128,128,128]{2,1,0:T(8,128)} %bitcast.14, f32[64,2048]{1,0:T(8,128)} %bitcast.11), custom_call_target="tpu_custom_call" | custom-call | flops 805306368 | bytes 8388608 | tf_op jit(solution)/shard_map/pallas_call | solution.py:258
  19.4 5.1 %all-to-all-start = ((f32[32,3,4,8,128]{4,3,2,1,0:T(8,128)}), f32[32,3,4,8,128]{4,3,2,1,0:T(8,128)S(1)}, u32[]{:S(2)}, u32[]{:S(2)}) async-start(f32[32,3,4,8,128]{4,3,2,1,0:T(8,128)} %get-tuple-element.59), calls=%async_computation | async-start | bytes 3145728 | tf_op jit(solution)/shard_map/all_to_all | solution.py:206
  24.5 8.0 %collective-permute-start.10 = (f32[8,4,8,128]{3,2,1,0:T(8,128)S(1)}, f32[8,4,8,128]{3,2,1,0:T(8,128)S(1)}, u32[]{:S(2)}, u32[]{:S(2)}) collective-permute-start(f32[8,4,8,128]{3,2,1,0:T(8,128)S(1)} %shard_map.66.near_ref), channel_id=1, source_target_pairs={{0,8},{8,0},{1,9},{9,1},{2,10},{10,2},{3,11},{11,3},{4,12},{12,4},... | collective-permute-start | bytes 393224 | tf_op jit(solution)/shard_map/ppermute | solution.py:268
  32.5 1.4 %collective-permute-start.9 = (s32[1,3]{1,0:T(1,128)S(1)}, s32[1,3]{1,0:T(1,128)S(1)}, u32[]{:S(2)}, u32[]{:S(2)}) collective-permute-start(s32[1,3]{1,0:T(1,128)S(1)} %copy-done.2), channel_id=1, source_target_pairs={{0,16},{16,32},{32,48},{48,0},{1,17},{17,33},{33,49},{49,1},{2,18}... | collective-permute-start | bytes 44 | tf_op jit(solution)/shard_map/ppermute | solution.py:255
  33.9 2.4 %collective-permute-start.8 = (s32[1,3]{1,0:T(1,128)S(1)}, s32[1,3]{1,0:T(1,128)S(1)}, u32[]{:S(2)}, u32[]{:S(2)}) collective-permute-start(s32[1,3]{1,0:T(1,128)S(1)} %copy-done.2), channel_id=1, source_target_pairs={{0,32},{16,48},{32,0},{48,16},{1,33},{17,49},{33,1},{49,17},{2,34}... | collective-permute-start | bytes 44 | tf_op jit(solution)/shard_map/ppermute | solution.py:255
  37.4 5.2 %collective-permute-done.9.m3 = s32[1,3]{1,0:T(1,128)S(1)} collective-permute-done((s32[1,3]{1,0:T(1,128)S(1)}, s32[1,3]{1,0:T(1,128)S(1)}, u32[]{:S(2)}, u32[]{:S(2)}) %collective-permute-start.9) | collective-permute-done | bytes 44 | tf_op jit(solution)/shard_map/ppermute | solution.py:255
  42.6 2.4 %collective-permute-done.8.m2 = s32[1,3]{1,0:T(1,128)S(1)} collective-permute-done((s32[1,3]{1,0:T(1,128)S(1)}, s32[1,3]{1,0:T(1,128)S(1)}, u32[]{:S(2)}, u32[]{:S(2)}) %collective-permute-start.8) | collective-permute-done | bytes 44 | tf_op jit(solution)/shard_map/ppermute | solution.py:255
  45.1 1.9 %shard_map.67 = f32[32,3,4,8,128]{4,3,2,1,0:T(8,128)} custom-call(s32[1]{0:T(128)} %bitcast.6.x_ref, s32[1]{0:T(128)} %bitcast.yc_ref, s32[1,3]{1,0:T(1,128)S(1)} %copy-done.2, s32[1,3]{1,0:T(1,128)S(1)} %collective-permute-done.7.m1, s32[1,3]{1,0:T(1,128)S(1)} %collective-permute-done.8.m2, s32[1,3]{1,0:T(1,128)S(1)} %collective-permute-done.9.m3, ...), custom_call_target="tpu_custom_call" | custom-call | tf_op jit(solution)/shard_map/pallas_call | solution.py:270
  47.2 5.8 %all-to-all-start.1 = ((f32[32,3,4,8,128]{4,3,2,1,0:T(8,128)}), f32[32,3,4,8,128]{4,3,2,1,0:T(8,128)S(1)}, u32[]{:S(2)}, u32[]{:S(2)}) async-start(f32[32,3,4,8,128]{4,3,2,1,0:T(8,128)} %shard_map.67), calls=%async_computation.1 | async-start | bytes 3145728 | tf_op jit(solution)/shard_map/all_to_all | solution.py:206
  54.1 8.0 %collective-permute-start.11 = (f32[4,8,8,128]{3,2,1,0:T(8,128)S(1)}, f32[4,8,8,128]{3,2,1,0:T(8,128)S(1)}, u32[]{:S(2)}, u32[]{:S(2)}) collective-permute-start(f32[4,8,8,128]{3,2,1,0:T(8,128)S(1)} %get-tuple-element.64), channel_id=1, source_target_pairs={{0,8},{8,0},{1,9},{9,1},{2,10},{10,2},{3,11},{11,3},{4,12},{12,4},... | collective-permute-start | bytes 393224 | tf_op jit(solution)/shard_map/ppermute | solution.py:287
  62.1 3.6 %collective-permute-done.11.b_ref = f32[4,8,8,128]{3,2,1,0:T(8,128)S(1)} collective-permute-done((f32[4,8,8,128]{3,2,1,0:T(8,128)S(1)}, f32[4,8,8,128]{3,2,1,0:T(8,128)S(1)}, u32[]{:S(2)}, u32[]{:S(2)}) %collective-permute-start.11) | collective-permute-done | bytes 131104 | tf_op jit(solution)/shard_map/ppermute | solution.py:287
  65.7 1.2 collective-permute-start.12
  66.9 6.0 %collective-permute-start.13 = (f32[8,8,128]{2,1,0:T(8,128)S(1)}, f32[8,8,128]{2,1,0:T(8,128)S(1)}, u32[]{:S(2)}, u32[]{:S(2)}) collective-permute-start(f32[8,8,128]{2,1,0:T(8,128)S(1)} %get-tuple-element.67), channel_id=1, source_target_pairs={{0,128},{64,192},{128,0},{192,64},{1,129},{65,193},{129,1},{193,65... | collective-permute-start | bytes 98312 | tf_op jit(solution)/shard_map/ppermute | solution.py:224
  73.0 1.7 %collective-permute-done.13.c_ref = f32[8,8,128]{2,1,0:T(8,128)S(1)} collective-permute-done((f32[8,8,128]{2,1,0:T(8,128)S(1)}, f32[8,8,128]{2,1,0:T(8,128)S(1)}, u32[]{:S(2)}, u32[]{:S(2)}) %collective-permute-start.13) | collective-permute-done | bytes 32800 | tf_op jit(solution)/shard_map/ppermute | solution.py:224
  74.8 2.8 %collective-permute-done.14.d_ref = f32[8,8,128]{2,1,0:T(8,128)S(1)} collective-permute-done((f32[8,8,128]{2,1,0:T(8,128)S(1)}, f32[8,8,128]{2,1,0:T(8,128)S(1)}, u32[]{:S(2)}, u32[]{:S(2)}) %collective-permute-start.14) | collective-permute-done | bytes 32800 | tf_op jit(solution)/shard_map/ppermute | solution.py:224
  78.7 6.5 %shard_map.71 = (f32[4,64,128]{2,1,0:T(8,128)}, f32[4,64,128]{2,1,0:T(8,128)}, f32[4,64,128]{2,1,0:T(8,128)}, f32[4,64,128]{2,1,0:T(8,128)}) custom-call(s32[1]{0:T(128)} %bitcast.6.x_ref, s32[128]{0:T(128)} %bitcast.17, s32[128]{0:T(128)} %bitcast.19, s32[1]{0:T(128)} %bitcast.10.count, f32[128,128,128]{2,1,0:T(8,128)} %bitcast.15, f32[64,2048]{1,0:T(8,128)} %bitcast.12, ...), custom_call_target="tpu_custom_call" | custom-call | flops 805306368 | bytes 8388608 | tf_op jit(solution)/shard_map/pallas_call | solution.py:293
  85.2 2.4 %collective-permute-start.22 = (f32[4,64,128]{2,1,0:T(8,128)}, f32[4,64,128]{2,1,0:T(8,128)S(1)}, u32[]{:S(2)}, u32[]{:S(2)}) collective-permute-start(f32[4,64,128]{2,1,0:T(8,128)} %get-tuple-element.88), channel_id=1, source_target_pairs={{0,16},{16,32},{32,48},{48,0},{1,17},{17,33},{33,49},{49,1},{2,18}... | collective-permute-start | bytes 393224 | tf_op jit(solution)/shard_map/ppermute | solution.py:302
  87.6 2.5 %collective-permute-start.24 = (f32[4,64,128]{2,1,0:T(8,128)}, f32[4,64,128]{2,1,0:T(8,128)S(1)}, u32[]{:S(2)}, u32[]{:S(2)}) collective-permute-start(f32[4,64,128]{2,1,0:T(8,128)} %get-tuple-element.90), channel_id=1, source_target_pairs={{0,48},{16,0},{32,16},{48,32},{1,49},{17,1},{33,17},{49,33},{2,50}... | collective-permute-start | bytes 393224 | tf_op jit(solution)/shard_map/ppermute | solution.py:302
  90.6 2.6 %collective-permute-done.23.c_ref = f32[4,64,128]{2,1,0:T(8,128)S(1)} collective-permute-done((f32[4,64,128]{2,1,0:T(8,128)}, f32[4,64,128]{2,1,0:T(8,128)S(1)}, u32[]{:S(2)}, u32[]{:S(2)}) %collective-permute-start.23) | collective-permute-done | bytes 131104 | tf_op jit(solution)/shard_map/ppermute | solution.py:302
  94.1 2.8 %collective-permute-start.25 = (f32[64,128]{1,0:T(8,128)S(1)}, f32[64,128]{1,0:T(8,128)S(1)}, u32[]{:S(2)}, u32[]{:S(2)}) collective-permute-start(f32[64,128]{1,0:T(8,128)S(1)} %get-tuple-element.92), channel_id=1, source_target_pairs={{0,64},{64,0},{128,192},{192,128},{1,65},{65,1},{129,193},{193,129... | collective-permute-start | bytes 98312 | tf_op jit(solution)/shard_map/ppermute | solution.py:224
  96.9 5.2 %collective-permute-start.26 = (f32[64,128]{1,0:T(8,128)S(1)}, f32[64,128]{1,0:T(8,128)S(1)}, u32[]{:S(2)}, u32[]{:S(2)}) collective-permute-start(f32[64,128]{1,0:T(8,128)S(1)} %get-tuple-element.93), channel_id=1, source_target_pairs={{0,128},{64,192},{128,0},{192,64},{1,129},{65,193},{129,1},{193,65... | collective-permute-start | bytes 98312 | tf_op jit(solution)/shard_map/ppermute | solution.py:224
  102.2 3.4 %collective-permute-start.15 = (f32[8,128]{1,0:T(8,128)S(1)}, f32[8,128]{1,0:T(8,128)S(1)}, u32[]{:S(2)}, u32[]{:S(2)}) collective-permute-start(f32[8,128]{1,0:T(8,128)S(1)} %get-tuple-element.78), channel_id=1, source_target_pairs={{0,1},{1,0},{2,3},{3,2},{4,5},{5,4},{6,7},{7,6},{8,9},{9,8},{10,11... | collective-permute-start | bytes 12296 | tf_op jit(solution)/shard_map/ppermute | solution.py:224
  108.3 1.7 %collective-permute-start.18 = (f32[8,128]{1,0:T(8,128)S(1)}, f32[8,128]{1,0:T(8,128)S(1)}, u32[]{:S(2)}, u32[]{:S(2)}) collective-permute-start(f32[8,128]{1,0:T(8,128)S(1)} %get-tuple-element.81), channel_id=1, source_target_pairs={{0,4},{1,5},{2,6},{3,7},{4,0},{5,1},{6,2},{7,3},{8,12},{9,13},{10,... | collective-permute-start | bytes 12296 | tf_op jit(solution)/shard_map/ppermute | solution.py:224
  110.0 2.3 %collective-permute-start.19 = (f32[8,128]{1,0:T(8,128)S(1)}, f32[8,128]{1,0:T(8,128)S(1)}, u32[]{:S(2)}, u32[]{:S(2)}) collective-permute-start(f32[8,128]{1,0:T(8,128)S(1)} %get-tuple-element.82), channel_id=1, source_target_pairs={{0,5},{1,4},{2,7},{3,6},{4,1},{5,0},{6,3},{7,2},{8,13},{9,12},{10,... | collective-permute-start | bytes 12296 | tf_op jit(solution)/shard_map/ppermute | solution.py:224
  112.9 1.7 %collective-permute-done.19.refs_5_ = f32[8,128]{1,0:T(8,128)S(1)} collective-permute-done((f32[8,128]{1,0:T(8,128)S(1)}, f32[8,128]{1,0:T(8,128)S(1)}, u32[]{:S(2)}, u32[]{:S(2)}) %collective-permute-start.19) | collective-permute-done | bytes 4128 | tf_op jit(solution)/shard_map/ppermute | solution.py:224
  114.6 2.6 %collective-permute-start.21 = (f32[8,128]{1,0:T(8,128)S(1)}, f32[8,128]{1,0:T(8,128)S(1)}, u32[]{:S(2)}, u32[]{:S(2)}) collective-permute-start(f32[8,128]{1,0:T(8,128)S(1)} %get-tuple-element.84), channel_id=1, source_target_pairs={{0,7},{1,6},{2,5},{3,4},{4,3},{5,2},{6,1},{7,0},{8,15},{9,14},{10,... | collective-permute-start | bytes 12296 | tf_op jit(solution)/shard_map/ppermute | solution.py:224
  117.1 1.7 %collective-permute-done.21.refs_7_ = f32[8,128]{1,0:T(8,128)S(1)} collective-permute-done((f32[8,128]{1,0:T(8,128)S(1)}, f32[8,128]{1,0:T(8,128)S(1)}, u32[]{:S(2)}, u32[]{:S(2)}) %collective-permute-start.21) | collective-permute-done | bytes 4128 | tf_op jit(solution)/shard_map/ppermute | solution.py:224
  (46 shorter events, 11.3 us)
Async XLA Ops:
  1.1 8.9 %collective-permute-start = (f32[4,8,128]{2,1,0:T(8,128)S(1)}, f32[4,8,128]{2,1,0:T(8,128)S(1)}, u32[]{:S(2)}, u32[]{:S(2)}) collective-permute-start(f32[4,8,128]{2,1,0:T(8,128)S(1)} %get-tuple-element.52), channel_id=1, source_target_pairs={{0,1},{1,0},{2,3},{3,2},{4,5},{5,4},{6,7},{7,6},{8,9},{9,8},{10,11... | collective-permute-start | bytes 49160 | tf_op jit(solution)/shard_map/ppermute | solution.py:224
  4.4 6.8 %collective-permute-start.1 = (f32[4,8,128]{2,1,0:T(8,128)S(1)}, f32[4,8,128]{2,1,0:T(8,128)S(1)}, u32[]{:S(2)}, u32[]{:S(2)}) collective-permute-start(f32[4,8,128]{2,1,0:T(8,128)S(1)} %get-tuple-element.53), channel_id=1, source_target_pairs={{0,2},{1,3},{2,0},{3,1},{4,6},{5,7},{6,4},{7,5},{8,10},{9,11},{10,... | collective-permute-start | bytes 49160 | tf_op jit(solution)/shard_map/ppermute | solution.py:224
  4.4 14.9 %collective-permute-start.2 = (f32[4,8,128]{2,1,0:T(8,128)S(1)}, f32[4,8,128]{2,1,0:T(8,128)S(1)}, u32[]{:S(2)}, u32[]{:S(2)}) collective-permute-start(f32[4,8,128]{2,1,0:T(8,128)S(1)} %get-tuple-element.54), channel_id=1, source_target_pairs={{0,3},{1,2},{2,1},{3,0},{4,7},{5,6},{6,5},{7,4},{8,11},{9,10},{10,... | collective-permute-start | bytes 49160 | tf_op jit(solution)/shard_map/ppermute | solution.py:224
  6.1 13.2 %collective-permute-start.3 = (f32[4,8,128]{2,1,0:T(8,128)S(1)}, f32[4,8,128]{2,1,0:T(8,128)S(1)}, u32[]{:S(2)}, u32[]{:S(2)}) collective-permute-start(f32[4,8,128]{2,1,0:T(8,128)S(1)} %get-tuple-element.55), channel_id=1, source_target_pairs={{0,4},{1,5},{2,6},{3,7},{4,0},{5,1},{6,2},{7,3},{8,12},{9,13},{10,... | collective-permute-start | bytes 49160 | tf_op jit(solution)/shard_map/ppermute | solution.py:224
  7.3 12.0 %collective-permute-start.4 = (f32[4,8,128]{2,1,0:T(8,128)S(1)}, f32[4,8,128]{2,1,0:T(8,128)S(1)}, u32[]{:S(2)}, u32[]{:S(2)}) collective-permute-start(f32[4,8,128]{2,1,0:T(8,128)S(1)} %get-tuple-element.56), channel_id=1, source_target_pairs={{0,5},{1,4},{2,7},{3,6},{4,1},{5,0},{6,3},{7,2},{8,13},{9,12},{10,... | collective-permute-start | bytes 49160 | tf_op jit(solution)/shard_map/ppermute | solution.py:224
  10.0 9.3 %collective-permute-start.5 = (f32[4,8,128]{2,1,0:T(8,128)S(1)}, f32[4,8,128]{2,1,0:T(8,128)S(1)}, u32[]{:S(2)}, u32[]{:S(2)}) collective-permute-start(f32[4,8,128]{2,1,0:T(8,128)S(1)} %get-tuple-element.57), channel_id=1, source_target_pairs={{0,6},{1,7},{2,4},{3,5},{4,2},{5,3},{6,0},{7,1},{8,14},{9,15},{10,... | collective-permute-start | bytes 49160 | tf_op jit(solution)/shard_map/ppermute | solution.py:224
  11.1 8.2 %collective-permute-start.6 = (f32[4,8,128]{2,1,0:T(8,128)S(1)}, f32[4,8,128]{2,1,0:T(8,128)S(1)}, u32[]{:S(2)}, u32[]{:S(2)}) collective-permute-start(f32[4,8,128]{2,1,0:T(8,128)S(1)} %get-tuple-element.58), channel_id=1, source_target_pairs={{0,7},{1,6},{2,5},{3,4},{4,3},{5,2},{6,1},{7,0},{8,15},{9,14},{10,... | collective-permute-start | bytes 49160 | tf_op jit(solution)/shard_map/ppermute | solution.py:224
  19.4 13.1 %copy-start.2 = (s32[1,3]{1,0:T(1,128)S(1)}, s32[1,3]{1,0:T(1,128)}, u32[]{:S(2)}) copy-start(s32[1,3]{1,0:T(1,128)} %m0.3) | copy-start | bytes 40
  19.4 27.8 %all-to-all-start = ((f32[32,3,4,8,128]{4,3,2,1,0:T(8,128)}), f32[32,3,4,8,128]{4,3,2,1,0:T(8,128)S(1)}, u32[]{:S(2)}, u32[]{:S(2)}) async-start(f32[32,3,4,8,128]{4,3,2,1,0:T(8,128)} %get-tuple-element.59), calls=%async_computation | async-start | bytes 3145728 | tf_op jit(solution)/shard_map/all_to_all | solution.py:206
  24.5 20.5 %collective-permute-start.10 = (f32[8,4,8,128]{3,2,1,0:T(8,128)S(1)}, f32[8,4,8,128]{3,2,1,0:T(8,128)S(1)}, u32[]{:S(2)}, u32[]{:S(2)}) collective-permute-start(f32[8,4,8,128]{3,2,1,0:T(8,128)S(1)} %shard_map.66.near_ref), channel_id=1, source_target_pairs={{0,8},{8,0},{1,9},{9,1},{2,10},{10,2},{3,11},{11,3},{4,12},{12,4},... | collective-permute-start | bytes 393224 | tf_op jit(solution)/shard_map/ppermute | solution.py:268
  32.5 10.1 %collective-permute-start.9 = (s32[1,3]{1,0:T(1,128)S(1)}, s32[1,3]{1,0:T(1,128)S(1)}, u32[]{:S(2)}, u32[]{:S(2)}) collective-permute-start(s32[1,3]{1,0:T(1,128)S(1)} %copy-done.2), channel_id=1, source_target_pairs={{0,16},{16,32},{32,48},{48,0},{1,17},{17,33},{33,49},{49,1},{2,18}... | collective-permute-start | bytes 44 | tf_op jit(solution)/shard_map/ppermute | solution.py:255
  33.9 11.2 %collective-permute-start.8 = (s32[1,3]{1,0:T(1,128)S(1)}, s32[1,3]{1,0:T(1,128)S(1)}, u32[]{:S(2)}, u32[]{:S(2)}) collective-permute-start(s32[1,3]{1,0:T(1,128)S(1)} %copy-done.2), channel_id=1, source_target_pairs={{0,32},{16,48},{32,0},{48,16},{1,33},{17,49},{33,1},{49,17},{2,34}... | collective-permute-start | bytes 44 | tf_op jit(solution)/shard_map/ppermute | solution.py:255
  36.3 8.7 %collective-permute-start.7 = (s32[1,3]{1,0:T(1,128)S(1)}, s32[1,3]{1,0:T(1,128)S(1)}, u32[]{:S(2)}, u32[]{:S(2)}) collective-permute-start(s32[1,3]{1,0:T(1,128)S(1)} %copy-done.2), channel_id=1, source_target_pairs={{0,48},{16,0},{32,16},{48,32},{1,49},{17,1},{33,17},{49,33},{2,50}... | collective-permute-start | bytes 44 | tf_op jit(solution)/shard_map/ppermute | solution.py:255
  47.2 30.4 %all-to-all-start.1 = ((f32[32,3,4,8,128]{4,3,2,1,0:T(8,128)}), f32[32,3,4,8,128]{4,3,2,1,0:T(8,128)S(1)}, u32[]{:S(2)}, u32[]{:S(2)}) async-start(f32[32,3,4,8,128]{4,3,2,1,0:T(8,128)} %shard_map.67), calls=%async_computation.1 | async-start | bytes 3145728 | tf_op jit(solution)/shard_map/all_to_all | solution.py:206
  54.1 11.6 %collective-permute-start.11 = (f32[4,8,8,128]{3,2,1,0:T(8,128)S(1)}, f32[4,8,8,128]{3,2,1,0:T(8,128)S(1)}, u32[]{:S(2)}, u32[]{:S(2)}) collective-permute-start(f32[4,8,8,128]{3,2,1,0:T(8,128)S(1)} %get-tuple-element.64), channel_id=1, source_target_pairs={{0,8},{8,0},{1,9},{9,1},{2,10},{10,2},{3,11},{11,3},{4,12},{12,4},... | collective-permute-start | bytes 393224 | tf_op jit(solution)/shard_map/ppermute | solution.py:287
  65.7 7.3 %collective-permute-start.12 = (f32[8,8,128]{2,1,0:T(8,128)S(1)}, f32[8,8,128]{2,1,0:T(8,128)S(1)}, u32[]{:S(2)}, u32[]{:S(2)}) collective-permute-start(f32[8,8,128]{2,1,0:T(8,128)S(1)} %get-tuple-element.66), channel_id=1, source_target_pairs={{0,64},{64,0},{128,192},{192,128},{1,65},{65,1},{129,193},{193,129... | collective-permute-start | bytes 98312 | tf_op jit(solution)/shard_map/ppermute | solution.py:224
  66.9 7.9 %collective-permute-start.13 = (f32[8,8,128]{2,1,0:T(8,128)S(1)}, f32[8,8,128]{2,1,0:T(8,128)S(1)}, u32[]{:S(2)}, u32[]{:S(2)}) collective-permute-start(f32[8,8,128]{2,1,0:T(8,128)S(1)} %get-tuple-element.67), channel_id=1, source_target_pairs={{0,128},{64,192},{128,0},{192,64},{1,129},{65,193},{129,1},{193,65... | collective-permute-start | bytes 98312 | tf_op jit(solution)/shard_map/ppermute | solution.py:224
  72.9 4.6 %collective-permute-start.14 = (f32[8,8,128]{2,1,0:T(8,128)S(1)}, f32[8,8,128]{2,1,0:T(8,128)S(1)}, u32[]{:S(2)}, u32[]{:S(2)}) collective-permute-start(f32[8,8,128]{2,1,0:T(8,128)S(1)} %get-tuple-element.68), channel_id=1, source_target_pairs={{0,192},{64,128},{128,64},{192,0},{1,193},{65,129},{129,65},{193,1... | collective-permute-start | bytes 98312 | tf_op jit(solution)/shard_map/ppermute | solution.py:224
  77.5 1.2 copy-start.3
  85.2 5.3 %collective-permute-start.22 = (f32[4,64,128]{2,1,0:T(8,128)}, f32[4,64,128]{2,1,0:T(8,128)S(1)}, u32[]{:S(2)}, u32[]{:S(2)}) collective-permute-start(f32[4,64,128]{2,1,0:T(8,128)} %get-tuple-element.88), channel_id=1, source_target_pairs={{0,16},{16,32},{32,48},{48,0},{1,17},{17,33},{33,49},{49,1},{2,18}... | collective-permute-start | bytes 393224 | tf_op jit(solution)/shard_map/ppermute | solution.py:302
  87.6 5.5 %collective-permute-start.23 = (f32[4,64,128]{2,1,0:T(8,128)}, f32[4,64,128]{2,1,0:T(8,128)S(1)}, u32[]{:S(2)}, u32[]{:S(2)}) collective-permute-start(f32[4,64,128]{2,1,0:T(8,128)} %get-tuple-element.89), channel_id=1, source_target_pairs={{0,32},{16,48},{32,0},{48,16},{1,33},{17,49},{33,1},{49,17},{2,34}... | collective-permute-start | bytes 393224 | tf_op jit(solution)/shard_map/ppermute | solution.py:302
  87.6 5.5 %collective-permute-start.24 = (f32[4,64,128]{2,1,0:T(8,128)}, f32[4,64,128]{2,1,0:T(8,128)S(1)}, u32[]{:S(2)}, u32[]{:S(2)}) collective-permute-start(f32[4,64,128]{2,1,0:T(8,128)} %get-tuple-element.90), channel_id=1, source_target_pairs={{0,48},{16,0},{32,16},{48,32},{1,49},{17,1},{33,17},{49,33},{2,50}... | collective-permute-start | bytes 393224 | tf_op jit(solution)/shard_map/ppermute | solution.py:302
  94.1 24.7 %collective-permute-start.25 = (f32[64,128]{1,0:T(8,128)S(1)}, f32[64,128]{1,0:T(8,128)S(1)}, u32[]{:S(2)}, u32[]{:S(2)}) collective-permute-start(f32[64,128]{1,0:T(8,128)S(1)} %get-tuple-element.92), channel_id=1, source_target_pairs={{0,64},{64,0},{128,192},{192,128},{1,65},{65,1},{129,193},{193,129... | collective-permute-start | bytes 98312 | tf_op jit(solution)/shard_map/ppermute | solution.py:224
  96.9 21.9 %collective-permute-start.26 = (f32[64,128]{1,0:T(8,128)S(1)}, f32[64,128]{1,0:T(8,128)S(1)}, u32[]{:S(2)}, u32[]{:S(2)}) collective-permute-start(f32[64,128]{1,0:T(8,128)S(1)} %get-tuple-element.93), channel_id=1, source_target_pairs={{0,128},{64,192},{128,0},{192,64},{1,129},{65,193},{129,1},{193,65... | collective-permute-start | bytes 98312 | tf_op jit(solution)/shard_map/ppermute | solution.py:224
  102.2 16.6 %collective-permute-start.27 = (f32[64,128]{1,0:T(8,128)S(1)}, f32[64,128]{1,0:T(8,128)S(1)}, u32[]{:S(2)}, u32[]{:S(2)}) collective-permute-start(f32[64,128]{1,0:T(8,128)S(1)} %get-tuple-element.94), channel_id=1, source_target_pairs={{0,192},{64,128},{128,64},{192,0},{1,193},{65,129},{129,65},{193,1... | collective-permute-start | bytes 98312 | tf_op jit(solution)/shard_map/ppermute | solution.py:224
  102.2 4.2 %collective-permute-start.15 = (f32[8,128]{1,0:T(8,128)S(1)}, f32[8,128]{1,0:T(8,128)S(1)}, u32[]{:S(2)}, u32[]{:S(2)}) collective-permute-start(f32[8,128]{1,0:T(8,128)S(1)} %get-tuple-element.78), channel_id=1, source_target_pairs={{0,1},{1,0},{2,3},{3,2},{4,5},{5,4},{6,7},{7,6},{8,9},{9,8},{10,11... | collective-permute-start | bytes 12296 | tf_op jit(solution)/shard_map/ppermute | solution.py:224
  105.5 2.8 %collective-permute-start.16 = (f32[8,128]{1,0:T(8,128)S(1)}, f32[8,128]{1,0:T(8,128)S(1)}, u32[]{:S(2)}, u32[]{:S(2)}) collective-permute-start(f32[8,128]{1,0:T(8,128)S(1)} %get-tuple-element.79), channel_id=1, source_target_pairs={{0,2},{1,3},{2,0},{3,1},{4,6},{5,7},{6,4},{7,5},{8,10},{9,11},{10,... | collective-permute-start | bytes 12296 | tf_op jit(solution)/shard_map/ppermute | solution.py:224
  106.4 3.7 %collective-permute-start.17 = (f32[8,128]{1,0:T(8,128)S(1)}, f32[8,128]{1,0:T(8,128)S(1)}, u32[]{:S(2)}, u32[]{:S(2)}) collective-permute-start(f32[8,128]{1,0:T(8,128)S(1)} %get-tuple-element.80), channel_id=1, source_target_pairs={{0,3},{1,2},{2,1},{3,0},{4,7},{5,6},{6,5},{7,4},{8,11},{9,10},{10,... | collective-permute-start | bytes 12296 | tf_op jit(solution)/shard_map/ppermute | solution.py:224
  108.3 4.0 %collective-permute-start.18 = (f32[8,128]{1,0:T(8,128)S(1)}, f32[8,128]{1,0:T(8,128)S(1)}, u32[]{:S(2)}, u32[]{:S(2)}) collective-permute-start(f32[8,128]{1,0:T(8,128)S(1)} %get-tuple-element.81), channel_id=1, source_target_pairs={{0,4},{1,5},{2,6},{3,7},{4,0},{5,1},{6,2},{7,3},{8,12},{9,13},{10,... | collective-permute-start | bytes 12296 | tf_op jit(solution)/shard_map/ppermute | solution.py:224
  110.0 4.5 %collective-permute-start.19 = (f32[8,128]{1,0:T(8,128)S(1)}, f32[8,128]{1,0:T(8,128)S(1)}, u32[]{:S(2)}, u32[]{:S(2)}) collective-permute-start(f32[8,128]{1,0:T(8,128)S(1)} %get-tuple-element.82), channel_id=1, source_target_pairs={{0,5},{1,4},{2,7},{3,6},{4,1},{5,0},{6,3},{7,2},{8,13},{9,12},{10,... | collective-permute-start | bytes 12296 | tf_op jit(solution)/shard_map/ppermute | solution.py:224
  112.3 4.8 %collective-permute-start.20 = (f32[8,128]{1,0:T(8,128)S(1)}, f32[8,128]{1,0:T(8,128)S(1)}, u32[]{:S(2)}, u32[]{:S(2)}) collective-permute-start(f32[8,128]{1,0:T(8,128)S(1)} %get-tuple-element.83), channel_id=1, source_target_pairs={{0,6},{1,7},{2,4},{3,5},{4,2},{5,3},{6,0},{7,1},{8,14},{9,15},{10,... | collective-permute-start | bytes 12296 | tf_op jit(solution)/shard_map/ppermute | solution.py:224
  114.6 4.2 %collective-permute-start.21 = (f32[8,128]{1,0:T(8,128)S(1)}, f32[8,128]{1,0:T(8,128)S(1)}, u32[]{:S(2)}, u32[]{:S(2)}) collective-permute-start(f32[8,128]{1,0:T(8,128)S(1)} %get-tuple-element.84), channel_id=1, source_target_pairs={{0,7},{1,6},{2,5},{3,4},{4,3},{5,2},{6,1},{7,0},{8,15},{9,14},{10,... | collective-permute-start | bytes 12296 | tf_op jit(solution)/shard_map/ppermute | solution.py:224
  (2 other events, 1.9 us)

commit v3 on v1

--- a/solution.py
+++ b/solution.py
@@ -139,8 +139,8 @@
                 out_ref[x * YC + part, slot, zlo] = value[part * SUB : (part + 1) * SUB]
 
 
-def rows_kernel(x_ref, rows, cols, count, tiles, own_ref, far_ref, self_ref, *rest):
-    outs, (held, table, sums, sems) = rest[:X], rest[X:]
+def rows_kernel(zlo_ref, rows, cols, count, tiles, own_ref, far_ref, self_ref, *rest):
+    outs, (held, table, sums, sems) = rest[:ZLO], rest[ZLO:]
     copies = fetch(tiles, held, sems)
     sums[...] = self_ref[...]
     vecs = own_ref.shape[0]
@@ -165,16 +165,23 @@
             sums[row] += done[k]
 
     each_group(copies, count[0], group)
+    for step in range(ZLO):
+        first = (zlo_ref[0] ^ step) * X
+        for x in range(X):
+            outs[step][x] = sums[first + x]
+
+
+def spread_kernel(x_ref, a_ref, b_ref, c_ref, d_ref, *outs):
     for step in range(X):
-        x = lax.rem(x_ref[0] + step, X)
-        for zlo in range(ZLO):
-            outs[step][zlo] = sums[zlo * X + x]
-
-
-def spread_kernel(zlo_ref, a_ref, b_ref, c_ref, d_ref, *outs):
-    for step in range(ZLO):
-        z = zlo_ref[0] ^ step
-        outs[step][...] = (a_ref[z] + b_ref[z]) + (c_ref[z] + d_ref[z])
+        x = x_ref[0] ^ step
+        outs[step][...] = (a_ref[x] + b_ref[x]) + (c_ref[x] + d_ref[x])
+
+
+def swaps(arrays, axis, count):
+    return [arrays[0]] + [
+        lax.ppermute(arrays[step], axis, [(i, i ^ step) for i in range(count)])
+        for step in range(1, count)
+    ]
 
 
 def exchange(value, axes):
@@ -233,34 +240,28 @@
         LARGE,
         half,
     )(*ids, tile_set, own)
-    parts = exchange(parts, FAN_AXES)
     (wanted,) = local(
         route_kernel, [(FAN, REGIONS - 1, *piece)], [SMEM] * 6 + [VMEM], limit=SMALL
     )(*where, pieces)
     far = exchange(wanted, FAN_AXES)
-    (sums,) = local(collect_kernel, [(ZLO, OWN, SUB, LANE)], [SMEM] * 6 + [VMEM], limit=SMALL)(
-        *where, parts
-    )
-    sums = exchange(sums.reshape(ZLO * OWN, SUB, LANE), OUT_AXES)
+    far, parts = lax.optimization_barrier((far, parts))
+    parts = exchange(parts, FAN_AXES)
     rows = local(
         rows_kernel,
-        [(ZLO, vecs, LANE)] * X,
+        [(X, vecs, LANE)] * ZLO,
         [SMEM] * 4 + [HBM, VMEM, VMEM, VMEM],
         tile_scratch(REGIONS * blocks, blocks),
         LARGE,
         half,
-    )(x, *ids, tile_set, own, far, mine)
-    rows = [rows[0]] + [
-        lax.ppermute(rows[step], "x", [(i, (i + step) % X) for i in range(X)])
-        for step in range(1, X)
-    ]
-    rows = local(spread_kernel, [(vecs, LANE)] * ZLO, [SMEM] + [VMEM] * X, limit=SMALL)(
-        zlo, *rows
-    )
-    rows = [rows[0]] + [
-        lax.ppermute(rows[step], "zlo", [(i, i ^ step) for i in range(ZLO)])
-        for step in range(1, ZLO)
-    ]
+    )(zlo, *ids, tile_set, own, far, mine)
+    rows = swaps(rows, "zlo", ZLO)
+    rows = local(spread_kernel, [(vecs, LANE)] * X, [SMEM] + [VMEM] * ZLO, limit=SMALL)(x, *rows)
+    parts, *rows = lax.optimization_barrier((parts, *rows))
+    (sums,) = local(collect_kernel, [(ZLO, OWN, SUB, LANE)], [SMEM] * 6 + [VMEM], limit=SMALL)(
+        *where, parts
+    )
+    sums = exchange(sums.reshape(ZLO * OWN, SUB, LANE), OUT_AXES)
+    rows = swaps(rows, "x", X)
     total = jnp.sum(sums.reshape(ZLO * ZHI, vecs, LANE), axis=0)
     for row in rows:
         total = total + row

time: 120 us -> 110 us (0.917)
  the two profiles are of different devices: /device:TPU:16 before, /device:TPU:1 now
where the time goes in v3:
time: 110 us
  starting transfers between devices  48.2 us (44%)
  waiting for transfers between devices  40.3 us (37%)
  Pallas kernels  16.2 us (15%)
  local copies, waits for them, and re-layouts  3.75 us (3%)
    all_to_all x4, starting transfers between devices, exchange(): return lax.all_to_all(value, axes, 0, 0, tiled=False)  33.5 us
    all_to_all x4, waiting for transfers between devices, exchange(): return lax.all_to_all(value, axes, 0, 0, tiled=False)  32.1 us
    ppermute x6, starting transfers between devices, swaps(): lax.ppermute(arrays[step], axis, [(i, i ^ step) for i in range(count)])  9.89 us
    ppermute x6, waiting for transfers between devices, swaps(): lax.ppermute(arrays[step], axis, [(i, i ^ step) for i in range(count)])  6.57 us
    pallas_call x1, Pallas kernels, on_device(): local(rows_kernel, [(X, vecs, LANE)] * ZLO, [SMEM] * 4 + [HBM, VMEM, VMEM...  5.99 us
    pallas_call x1, Pallas kernels, on_device(): local(columns_kernel, [(FAN, REGIONS - 1, *piece), (blocks, vecs, LANE)],...  5.92 us
    ppermute x3, starting transfers between devices, on_device(): lax.ppermute(matchings, 'x', [(i, (i - step) % X) for i in range(X)])  4.81 us
    unnamed x10, local copies, waits for them, and re-layouts  3.75 us
  transfers between devices with their start and end apart: 13, of which 9 were waited for; matrix products, arithmetic and copies ran while one was open for 0% of the time, Pallas kernels for 11%

profile of v3, /device:TPU:1, one launch (start us, length us, event | category | flops | bytes accessed | tf_op | source)
XLA Modules:
  0.0 109.9 jit_solution(17862642012641117608)
XLA Ops:
  0.0 1.0 copy-done
  1.0 0.7 pieces_kernel.1
  1.8 12.6 %all-to-all-start = ((f32[16,4,8,128]{3,2,1,0:T(8,128)}), f32[16,4,8,128]{3,2,1,0:T(8,128)S(1)}, u32[]{:S(2)}, u32[]{:S(2)}) async-start(f32[16,4,8,128]{3,2,1,0:T(8,128)} %pieces_kernel.1), calls=%async_computation | async-start | bytes 524288 | tf_op jit(solution)/shard_map/all_to_all | solution.py:188
  14.4 1.2 %collective-permute-start.2 = (s32[1,3]{1,0:T(1,128)}, s32[1,3]{1,0:T(1,128)S(1)}, u32[]{:S(2)}, u32[]{:S(2)}) collective-permute-start(s32[1,3]{1,0:T(1,128)} %m0.3), channel_id=1, source_target_pairs={{0,16},{16,32},{32,48},{48,0},{1,17},{17,33},{33,49},{49,1},{2,18}... | collective-permute-start | bytes 44 | tf_op jit(solution)/shard_map/ppermute | solution.py:215
  15.6 2.4 %collective-permute-start.1 = (s32[1,3]{1,0:T(1,128)}, s32[1,3]{1,0:T(1,128)S(1)}, u32[]{:S(2)}, u32[]{:S(2)}) collective-permute-start(s32[1,3]{1,0:T(1,128)} %m0.3), channel_id=1, source_target_pairs={{0,32},{16,48},{32,0},{48,16},{1,33},{17,49},{33,1},{49,17},{2,34}... | collective-permute-start | bytes 44 | tf_op jit(solution)/shard_map/ppermute | solution.py:215
  18.0 1.2 %collective-permute-start = (s32[1,3]{1,0:T(1,128)}, s32[1,3]{1,0:T(1,128)S(1)}, u32[]{:S(2)}, u32[]{:S(2)}) collective-permute-start(s32[1,3]{1,0:T(1,128)} %m0.3), channel_id=1, source_target_pairs={{0,48},{16,0},{32,16},{48,32},{1,49},{17,1},{33,17},{49,33},{2,50}... | collective-permute-start | bytes 44 | tf_op jit(solution)/shard_map/ppermute | solution.py:215
  19.2 0.5 collective-permute-done.1.m2
  19.6 1.2 %collective-permute-done.m1 = s32[1,3]{1,0:T(1,128)S(1)} collective-permute-done((s32[1,3]{1,0:T(1,128)}, s32[1,3]{1,0:T(1,128)S(1)}, u32[]{:S(2)}, u32[]{:S(2)}) %collective-permute-start) | collective-permute-done | bytes 44 | tf_op jit(solution)/shard_map/ppermute | solution.py:215
  20.9 4.6 %all-to-all-done.pieces_ref = f32[16,4,8,128]{3,2,1,0:T(8,128)S(1)} async-done(((f32[16,4,8,128]{3,2,1,0:T(8,128)}), f32[16,4,8,128]{3,2,1,0:T(8,128)S(1)}, u32[]{:S(2)}, u32[]{:S(2)}) %all-to-all-start) | async-done | bytes 262176 | tf_op jit(solution)/shard_map/all_to_all | solution.py:188
  25.5 0.7 copy-done.2
  26.2 1.8 %route_kernel.1 = f32[32,3,4,8,128]{4,3,2,1,0:T(8,128)} custom-call(s32[1]{0:T(128)} %bitcast.x_ref, s32[1]{0:T(128)} %bitcast.1.zhi_ref, s32[1,3]{1,0:T(1,128)S(1)} %copy-done.2, s32[1,3]{1,0:T(1,128)S(1)} %collective-permute-done.m1, s32[1,3]{1,0:T(1,128)S(1)} %collective-permute-done.1.m2, s32[1,3]{1,0:T(1,128)S(1)} %collective-permute-done.2.m3, ...), custom_call_target="tpu_custom_call" | custom-call | tf_op jit(solution)/shard_map/route_kernel/pallas_call | solution.py:243
  28.0 5.8 %all-to-all-start.1 = ((f32[32,3,4,8,128]{4,3,2,1,0:T(8,128)}), f32[32,3,4,8,128]{4,3,2,1,0:T(8,128)S(1)}, u32[]{:S(2)}, u32[]{:S(2)}) async-start(f32[32,3,4,8,128]{4,3,2,1,0:T(8,128)} %route_kernel.1), calls=%async_computation.1 | async-start | bytes 3145728 | tf_op jit(solution)/shard_map/all_to_all | solution.py:188
  34.5 5.9 %columns_kernel.1 = (f32[32,3,4,8,128]{4,3,2,1,0:T(8,128)}, f32[16,64,128]{2,1,0:T(8,128)}) custom-call(s32[128]{0:T(128)} %bitcast.22, s32[128]{0:T(128)} %bitcast.24, s32[1]{0:T(128)} %bitcast.14.count, f32[128,128,128]{2,1,0:T(8,128)} %bitcast.19, f32[64,2048]{1,0:T(8,128)} %bitcast.16), custom_call_target="tpu_custom_call" | custom-call | flops 805306368 | bytes 8388608 | tf_op jit(solution)/shard_map/columns_kernel/pallas_call | solution.py:235
  40.4 16.1 %all-to-all-done.1.far_ref = f32[32,3,4,8,128]{4,3,2,1,0:T(8,128)S(1)} async-done(((f32[32,3,4,8,128]{4,3,2,1,0:T(8,128)}), f32[32,3,4,8,128]{4,3,2,1,0:T(8,128)S(1)}, u32[]{:S(2)}, u32[]{:S(2)}) %all-to-all-start.1) | async-done | bytes 1572896 | tf_op jit(solution)/shard_map/all_to_all | solution.py:188
  56.5 1.1 %copy-done.4 = f32[32,3,4,8,128]{4,3,2,1,0:T(8,128)} copy-done((f32[32,3,4,8,128]{4,3,2,1,0:T(8,128)}, f32[32,3,4,8,128]{4,3,2,1,0:T(8,128)S(1)}, u32[]{:S(2)}) %copy-start.4) | copy-done | bytes 1572888
  57.6 4.2 %all-to-all-start.2 = ((f32[32,3,4,8,128]{4,3,2,1,0:T(8,128)}), f32[32,3,4,8,128]{4,3,2,1,0:T(8,128)S(1)}, u32[]{:S(2)}, u32[]{:S(2)}) async-start(f32[32,3,4,8,128]{4,3,2,1,0:T(8,128)} %get-tuple-element.23), calls=%async_computation.2 | async-start | bytes 3145728 | tf_op jit(solution)/shard_map/all_to_all | solution.py:188
  61.8 0.0 copy-start.3
  61.8 6.0 %rows_kernel.1 = (f32[4,64,128]{2,1,0:T(8,128)}, f32[4,64,128]{2,1,0:T(8,128)}, f32[4,64,128]{2,1,0:T(8,128)}, f32[4,64,128]{2,1,0:T(8,128)}) custom-call(s32[1]{0:T(128)} %bitcast.7.zlo_ref, s32[128]{0:T(128)} %bitcast.23, s32[128]{0:T(128)} %bitcast.25, s32[1]{0:T(128)} %bitcast.15.count, f32[128,128,128]{2,1,0:T(8,128)} %bitcast.20, f32[64,2048]{1,0:T(8,128)} %bitcast.17, ...), custom_call_target="tpu_custom_call" | custom-call | flops 805306368 | bytes 8388608 | tf_op jit(solution)/shard_map/rows_kernel/pallas_call | solution.py:249
  67.8 3.4 %collective-permute-start.3 = (f32[4,64,128]{2,1,0:T(8,128)}, f32[4,64,128]{2,1,0:T(8,128)S(1)}, u32[]{:S(2)}, u32[]{:S(2)}) collective-permute-start(f32[4,64,128]{2,1,0:T(8,128)} %get-tuple-element.27), channel_id=1, source_target_pairs={{0,64},{64,0},{128,192},{192,128},{1,65},{65,1},{129,193},{193,129... | collective-permute-start | bytes 393224 | tf_op jit(solution)/shard_map/ppermute | solution.py:182
  71.3 1.6 %collective-permute-start.4 = (f32[4,64,128]{2,1,0:T(8,128)}, f32[4,64,128]{2,1,0:T(8,128)S(1)}, u32[]{:S(2)}, u32[]{:S(2)}) collective-permute-start(f32[4,64,128]{2,1,0:T(8,128)} %get-tuple-element.28), channel_id=1, source_target_pairs={{0,128},{64,192},{128,0},{192,64},{1,129},{65,193},{129,1},{193,65... | collective-permute-start | bytes 393224 | tf_op jit(solution)/shard_map/ppermute | solution.py:182
  72.9 0.6 collective-permute-start.5
  73.4 0.4 collective-permute-done.3.b_ref
  73.8 5.2 %collective-permute-done.4.c_ref = f32[4,64,128]{2,1,0:T(8,128)S(1)} collective-permute-done((f32[4,64,128]{2,1,0:T(8,128)}, f32[4,64,128]{2,1,0:T(8,128)S(1)}, u32[]{:S(2)}, u32[]{:S(2)}) %collective-permute-start.4) | collective-permute-done | bytes 131104 | tf_op jit(solution)/shard_map/ppermute | solution.py:182
  79.0 1.0 collective-permute-done.5.d_ref
  80.0 0.9 copy-done.1
  80.9 3.6 %all-to-all-done.2.parts_ref = f32[32,3,4,8,128]{4,3,2,1,0:T(8,128)S(1)} async-done(((f32[32,3,4,8,128]{4,3,2,1,0:T(8,128)}), f32[32,3,4,8,128]{4,3,2,1,0:T(8,128)S(1)}, u32[]{:S(2)}, u32[]{:S(2)}) %all-to-all-start.2) | async-done | bytes 1572896 | tf_op jit(solution)/shard_map/all_to_all | solution.py:188
  84.6 1.7 %collect_kernel.1 = f32[4,16,8,128]{3,2,1,0:T(8,128)} custom-call(s32[1]{0:T(128)} %bitcast.x_ref, s32[1]{0:T(128)} %bitcast.1.zhi_ref, s32[1,3]{1,0:T(1,128)S(1)} %copy-done.3, s32[1,3]{1,0:T(1,128)S(1)} %collective-permute-done.m1, s32[1,3]{1,0:T(1,128)S(1)} %collective-permute-done.1.m2, s32[1,3]{1,0:T(1,128)S(1)} %collective-permute-done.2.m3, ...), custom_call_target="tpu_custom_call" | custom-call | tf_op jit(solution)/shard_map/collect_kernel/pallas_call | solution.py:260
  86.3 10.9 %all-to-all-start.3 = ((f32[64,8,128]{2,1,0:T(8,128)}), f32[64,8,128]{2,1,0:T(8,128)S(1)}, u32[]{:S(2)}, u32[]{:S(2)}) async-start(f32[64,8,128]{2,1,0:T(8,128)} %bitcast.8), calls=%async_computation.3 | async-start | bytes 524288 | tf_op jit(solution)/shard_map/all_to_all | solution.py:188
  97.2 0.1 collective-permute-start.6
  97.3 4.2 %collective-permute-start.7 = (f32[64,128]{1,0:T(8,128)S(1)}, f32[64,128]{1,0:T(8,128)S(1)}, u32[]{:S(2)}, u32[]{:S(2)}) collective-permute-start(f32[64,128]{1,0:T(8,128)S(1)} %get-tuple-element.37), channel_id=1, source_target_pairs={{0,32},{16,48},{32,0},{48,16},{1,33},{17,49},{33,1},{49,17},{2,34}... | collective-permute-start | bytes 98312 | tf_op jit(solution)/shard_map/ppermute | solution.py:182
  101.5 7.7 %all-to-all-done.3 = f32[64,8,128]{2,1,0:T(8,128)S(1)} async-done(((f32[64,8,128]{2,1,0:T(8,128)}), f32[64,8,128]{2,1,0:T(8,128)S(1)}, u32[]{:S(2)}, u32[]{:S(2)}) %all-to-all-start.3) | async-done | bytes 262176 | tf_op jit(solution)/shard_map/all_to_all | solution.py:188
  109.2 0.6 add_bitcast_fusion
  (12 shorter events, 0.1 us)
Async XLA Ops:
  0.0 1.0 copy-start
  1.8 23.7 %all-to-all-start = ((f32[16,4,8,128]{3,2,1,0:T(8,128)}), f32[16,4,8,128]{3,2,1,0:T(8,128)S(1)}, u32[]{:S(2)}, u32[]{:S(2)}) async-start(f32[16,4,8,128]{3,2,1,0:T(8,128)} %pieces_kernel.1), calls=%async_computation | async-start | bytes 524288 | tf_op jit(solution)/shard_map/all_to_all | solution.py:188
  14.4 4.8 %collective-permute-start.2 = (s32[1,3]{1,0:T(1,128)}, s32[1,3]{1,0:T(1,128)S(1)}, u32[]{:S(2)}, u32[]{:S(2)}) collective-permute-start(s32[1,3]{1,0:T(1,128)} %m0.3), channel_id=1, source_target_pairs={{0,16},{16,32},{32,48},{48,0},{1,17},{17,33},{33,49},{49,1},{2,18}... | collective-permute-start | bytes 44 | tf_op jit(solution)/shard_map/ppermute | solution.py:215
  15.6 4.1 %collective-permute-start.1 = (s32[1,3]{1,0:T(1,128)}, s32[1,3]{1,0:T(1,128)S(1)}, u32[]{:S(2)}, u32[]{:S(2)}) collective-permute-start(s32[1,3]{1,0:T(1,128)} %m0.3), channel_id=1, source_target_pairs={{0,32},{16,48},{32,0},{48,16},{1,33},{17,49},{33,1},{49,17},{2,34}... | collective-permute-start | bytes 44 | tf_op jit(solution)/shard_map/ppermute | solution.py:215
  18.0 2.8 %collective-permute-start = (s32[1,3]{1,0:T(1,128)}, s32[1,3]{1,0:T(1,128)S(1)}, u32[]{:S(2)}, u32[]{:S(2)}) collective-permute-start(s32[1,3]{1,0:T(1,128)} %m0.3), channel_id=1, source_target_pairs={{0,48},{16,0},{32,16},{48,32},{1,49},{17,1},{33,17},{49,33},{2,50}... | collective-permute-start | bytes 44 | tf_op jit(solution)/shard_map/ppermute | solution.py:215
  25.5 0.7 copy-start.2
  28.0 28.5 %all-to-all-start.1 = ((f32[32,3,4,8,128]{4,3,2,1,0:T(8,128)}), f32[32,3,4,8,128]{4,3,2,1,0:T(8,128)S(1)}, u32[]{:S(2)}, u32[]{:S(2)}) async-start(f32[32,3,4,8,128]{4,3,2,1,0:T(8,128)} %route_kernel.1), calls=%async_computation.1 | async-start | bytes 3145728 | tf_op jit(solution)/shard_map/all_to_all | solution.py:188
  56.5 1.1 %copy-start.4 = (f32[32,3,4,8,128]{4,3,2,1,0:T(8,128)}, f32[32,3,4,8,128]{4,3,2,1,0:T(8,128)S(1)}, u32[]{:S(2)}) copy-start(f32[32,3,4,8,128]{4,3,2,1,0:T(8,128)S(1)} %all-to-all-done.1.far_ref) | copy-start | bytes 4718596
  57.6 26.9 %all-to-all-start.2 = ((f32[32,3,4,8,128]{4,3,2,1,0:T(8,128)}), f32[32,3,4,8,128]{4,3,2,1,0:T(8,128)S(1)}, u32[]{:S(2)}, u32[]{:S(2)}) async-start(f32[32,3,4,8,128]{4,3,2,1,0:T(8,128)} %get-tuple-element.23), calls=%async_computation.2 | async-start | bytes 3145728 | tf_op jit(solution)/shard_map/all_to_all | solution.py:188
  61.8 22.8 %copy-start.3 = (s32[1,3]{1,0:T(1,128)S(1)}, s32[1,3]{1,0:T(1,128)}, u32[]{:S(2)}) copy-start(s32[1,3]{1,0:T(1,128)} %m0.3) | copy-start | bytes 40
  67.8 6.0 %collective-permute-start.3 = (f32[4,64,128]{2,1,0:T(8,128)}, f32[4,64,128]{2,1,0:T(8,128)S(1)}, u32[]{:S(2)}, u32[]{:S(2)}) collective-permute-start(f32[4,64,128]{2,1,0:T(8,128)} %get-tuple-element.27), channel_id=1, source_target_pairs={{0,64},{64,0},{128,192},{192,128},{1,65},{65,1},{129,193},{193,129... | collective-permute-start | bytes 393224 | tf_op jit(solution)/shard_map/ppermute | solution.py:182
  71.3 7.8 %collective-permute-start.4 = (f32[4,64,128]{2,1,0:T(8,128)}, f32[4,64,128]{2,1,0:T(8,128)S(1)}, u32[]{:S(2)}, u32[]{:S(2)}) collective-permute-start(f32[4,64,128]{2,1,0:T(8,128)} %get-tuple-element.28), channel_id=1, source_target_pairs={{0,128},{64,192},{128,0},{192,64},{1,129},{65,193},{129,1},{193,65... | collective-permute-start | bytes 393224 | tf_op jit(solution)/shard_map/ppermute | solution.py:182
  72.9 7.2 %collective-permute-start.5 = (f32[4,64,128]{2,1,0:T(8,128)}, f32[4,64,128]{2,1,0:T(8,128)S(1)}, u32[]{:S(2)}, u32[]{:S(2)}) collective-permute-start(f32[4,64,128]{2,1,0:T(8,128)} %get-tuple-element.29), channel_id=1, source_target_pairs={{0,192},{64,128},{128,64},{192,0},{1,193},{65,129},{129,65},{193,1... | collective-permute-start | bytes 393224 | tf_op jit(solution)/shard_map/ppermute | solution.py:182
  80.0 0.9 copy-start.1
  86.3 22.9 %all-to-all-start.3 = ((f32[64,8,128]{2,1,0:T(8,128)}), f32[64,8,128]{2,1,0:T(8,128)S(1)}, u32[]{:S(2)}, u32[]{:S(2)}) async-start(f32[64,8,128]{2,1,0:T(8,128)} %bitcast.8), calls=%async_computation.3 | async-start | bytes 524288 | tf_op jit(solution)/shard_map/all_to_all | solution.py:188
  97.2 12.0 %collective-permute-start.6 = (f32[64,128]{1,0:T(8,128)S(1)}, f32[64,128]{1,0:T(8,128)S(1)}, u32[]{:S(2)}, u32[]{:S(2)}) collective-permute-start(f32[64,128]{1,0:T(8,128)S(1)} %get-tuple-element.36), channel_id=1, source_target_pairs={{0,16},{16,0},{32,48},{48,32},{1,17},{17,1},{33,49},{49,33},{2,18}... | collective-permute-start | bytes 98312 | tf_op jit(solution)/shard_map/ppermute | solution.py:182
  97.3 11.9 %collective-permute-start.7 = (f32[64,128]{1,0:T(8,128)S(1)}, f32[64,128]{1,0:T(8,128)S(1)}, u32[]{:S(2)}, u32[]{:S(2)}) collective-permute-start(f32[64,128]{1,0:T(8,128)S(1)} %get-tuple-element.37), channel_id=1, source_target_pairs={{0,32},{16,48},{32,0},{48,16},{1,33},{17,49},{33,1},{49,17},{2,34}... | collective-permute-start | bytes 98312 | tf_op jit(solution)/shard_map/ppermute | solution.py:182
  101.5 7.8 %collective-permute-start.8 = (f32[64,128]{1,0:T(8,128)S(1)}, f32[64,128]{1,0:T(8,128)S(1)}, u32[]{:S(2)}, u32[]{:S(2)}) collective-permute-start(f32[64,128]{1,0:T(8,128)S(1)} %get-tuple-element.38), channel_id=1, source_target_pairs={{0,48},{16,32},{32,16},{48,0},{1,49},{17,33},{33,17},{49,1},{2,50}... | collective-permute-start | bytes 98312 | tf_op jit(solution)/shard_map/ppermute | solution.py:182
